TPU v7x, 32 devices: a whole 2x2x4 slice. The times are simulated.
32 devices in a mesh: groups: 2 (over y), det: 4 (over z), blk: 2 (over x), sub: 2 (over core).
Axes of the slice: x: 2, y: 2, z: 4, core: 2. Of those that a mesh axis runs over, the one named last changes fastest.
Arguments:
- tod: float32 [256, 4, 1024], P(('groups', 'det'), None, ('blk', 'sub')), parts along dimension 0, may hold values from -30 to 30
- pixels: int32 [256, 4, 1024], P('groups', 'det', ('blk', 'sub')), parts along dimension 0, may hold values from 0 to 3071
- span_block: int32 [8, 8], P('groups', ('blk', 'sub')), parts along dimension 0, may hold values from 0 to 7
- weight_class: int32 [256], P('groups'), parts along dimension 0, may hold values from 0 to 7
- class_weight: float32 [16], P('groups'), parts along dimension 0, may hold values from 0.25 to 4
Outputs:
- signal_sum: float32 [16, 3072], P(('groups', 'blk'), ('det', 'sub')), parts along dimension 0
- weight_sum: float32 [16, 3072], P(('groups', 'blk'), ('det', 'sub')), parts along dimension 0
- hit_count: float32 [16, 3072], P(('groups', 'blk'), ('det', 'sub')), parts along dimension 0
There are 2 independent parts, one for each index of `groups`. A program takes and returns all parts, laid end to end along the dimension named above; each array names one. Nothing has to cross between parts.
All inputs are finite; a program needn't handle non-finite values.
Results may differ from a plain program's by a relative error of at most 0.005.
Values sent between devices are 32-bit elements; how exact they have to be, the bound alone decides.
No kernel may reach another device: no remote copies, remote signals or barrier semaphores. Data moves between devices by JAX's collectives and lax.ppermute only.
A program may use at most 64 MiB of HBM per device.

v0:
```python
import jax
import jax.numpy as jnp
from jax import lax
from jax.sharding import PartitionSpec as P

BLOCK_PIX = 3072
SPAN = 128
BLK_OWN = 4


def on_device(tod, pixels, span_block, weight_class, class_weight):
    classes = class_weight.shape[0]
    picker = (weight_class[:, None] == jnp.arange(classes, dtype=jnp.int32)[None, :]).astype(
        jnp.float32
    )
    weight = jnp.sum(picker * class_weight[None, :], axis=1)
    total = jnp.sum(weight)
    regrouped = lax.all_to_all(tod, "det", split_axis=1, concat_axis=0, tiled=True)
    common = jnp.sum(weight[:, None, None] * regrouped, axis=0, keepdims=True) / total
    values = (weight[:, None, None] * (regrouped - common)).astype(jnp.bfloat16)
    detectors = values.shape[0]
    samples = values.shape[2]
    spans = samples // SPAN
    groups = 4
    size_group = detectors // groups
    turns = groups * spans
    own_row = lax.dynamic_slice_in_dim(span_block, lax.axis_index("det"), 1, 0)[0]
    values = (
        values.reshape(groups, size_group, spans, SPAN)
        .transpose(0, 2, 1, 3)
        .reshape(turns, size_group, SPAN)
    )
    where = (
        pixels.reshape(groups, size_group, spans, SPAN)
        .transpose(0, 2, 1, 3)
        .reshape(turns, size_group, SPAN)
    )
    weight_low = weight.astype(jnp.bfloat16).reshape(groups, 1, size_group)
    weight_low = jnp.broadcast_to(weight_low, (groups, spans, size_group)).reshape(
        turns, size_group
    )
    span_of = jnp.broadcast_to(
        jnp.arange(spans, dtype=jnp.int32)[None, :], (groups, spans)
    ).reshape(turns)
    lanes = 128
    upper = BLOCK_PIX // lanes
    nblocks = BLK_OWN * lax.axis_size("blk")
    count = size_group * SPAN
    selector = (span_of[:, None] == jnp.arange(spans, dtype=jnp.int32)[None, :]).astype(jnp.float32)

    def bin_tile(total_map, item):
        tile_values, tile_pixels, tile_weight, select = item
        high = tile_pixels // lanes
        low = tile_pixels % lanes
        high_hot = (high[..., None] == jnp.arange(upper, dtype=jnp.int32)).astype(jnp.bfloat16)
        first = tile_values[..., None] * high_hot
        second = tile_weight[:, None, None] * high_hot
        stacked = jnp.concatenate([first, second, high_hot], axis=-1).reshape(count, 3 * upper)
        low_hot = (
            (low[..., None] == jnp.arange(lanes, dtype=jnp.int32))
            .astype(jnp.bfloat16)
            .reshape(count, lanes)
        )
        binned = lax.dot_general(
            stacked, low_hot, (((0,), (0,)), ((), ())), preferred_element_type=jnp.float32
        )
        return (total_map + select[:, None, None] * binned[None], None)

    start = jnp.zeros((spans, 3 * upper, lanes), jnp.float32)
    binned_map, unused = lax.scan(bin_tile, start, (values, where, weight_low, selector))
    binned_map = binned_map.reshape(spans, 3, BLOCK_PIX)
    count_det = lax.axis_size("det")
    count_sub = lax.axis_size("sub")
    peers = count_det * count_sub
    width = BLOCK_PIX // peers
    pieces = binned_map.reshape(spans, 3, peers, width)
    labels = jnp.broadcast_to(
        own_row.astype(jnp.float32)[:, None, None, None], (spans, 1, peers, 1)
    )
    received, got_labels = (
        lax.all_to_all(pieces, ("det", "sub"), split_axis=2, concat_axis=0, tiled=True),
        lax.all_to_all(labels, ("det", "sub"), split_axis=2, concat_axis=0, tiled=True),
    )
    received = received.reshape(peers * spans, 3 * width)
    got_labels = got_labels.reshape(peers * spans)
    placing = (got_labels[:, None] == jnp.arange(nblocks, dtype=jnp.float32)[None, :]).astype(
        jnp.float32
    )
    gathered = lax.dot_general(
        placing,
        received,
        (((0,), (0,)), ((), ())),
        precision=lax.Precision.HIGHEST,
        preferred_element_type=jnp.float32,
    )
    gathered = gathered.reshape(nblocks, 3, width)
    mine = lax.psum_scatter(gathered, "blk", scatter_dimension=0, tiled=True)
    signal_sum, weight_sum, hit_count = (mine[:, 0], mine[:, 1], mine[:, 2])
    return (signal_sum, weight_sum, hit_count)


def solution(mesh):
    placed = (
        P(("groups", "det"), None, ("blk", "sub")),
        P("groups", "det", ("blk", "sub")),
        P("groups", ("blk", "sub")),
        P("groups"),
        P("groups"),
    )
    return jax.shard_map(
        on_device,
        mesh=mesh,
        in_specs=placed,
        out_specs=(
            P(("groups", "blk"), ("det", "sub")),
            P(("groups", "blk"), ("det", "sub")),
            P(("groups", "blk"), ("det", "sub")),
        ),
        check_vma=False,
    )
```

profile of v0, /device:TPU:0, one launch (start us, length us, event | category | flops | bytes accessed | tf_op | source)
XLA Modules:
  0.0 50.1 jit_solution(9082960590155810975)
XLA Ops:
  0.6 1.6 %copy.35 = f32[32,4,256]{2,0,1:T(8,128)} copy(f32[32,4,256]{2,1,0:T(4,128)} %param.7) | data formatting | bytes 262144 | tf_op args[0]
  2.2 6.5 %all-to-all-start.1 = ((f32[32,4,256]{2,0,1:T(8,128)}), f32[32,4,256]{2,0,1:T(8,128)S(1)}, u32[]{:S(2)}, u32[]{:S(2)}) async-start(f32[32,4,256]{2,0,1:T(8,128)} %copy.35), calls=%async_computation.1 | async-start | bytes 262144 | tf_op jit(solution)/shard_map/all_to_all | solution.py:18
  8.7 0.7 %select_reduce_fusion = (f32[]{:T(128)}, f32[128]{0:T(128)S(1)}) fusion(f32[8]{0:T(128)S(1)} %copy-done.2, s32[128]{0:T(128)S(1)} %copy-done.3), kind=kLoop, calls=%fused_computation.40 | loop fusion | flops 3967 | bytes 1060 | tf_op jit(solution)/shard_map/reduce_sum | solution.py:17
  9.4 0.1 mul.98
  9.5 0.1 eq.91
  9.6 0.2 convert_reduce_fusion
  9.8 0.1 fusion.24
  9.8 4.9 %all-to-all-done.1 = f32[32,4,256]{2,0,1:T(8,128)S(1)} async-done(((f32[32,4,256]{2,0,1:T(8,128)}), f32[32,4,256]{2,0,1:T(8,128)S(1)}, u32[]{:S(2)}, u32[]{:S(2)}) %all-to-all-start.1) | async-done | bytes 131104 | tf_op jit(solution)/shard_map/all_to_all | solution.py:18
  14.8 0.6 %broadcast_in_dim.8 = f32[2,1,8,1]{0,3,1,2:T(1,128)} broadcast(f32[2]{0:T(128)S(1)} %convert_reduce_fusion), dimensions={0} | broadcast | bytes 72 | tf_op jit(solution)/shard_map/broadcast_in_dim | solution.py:77
  15.3 3.3 %all-to-all-start = ((f32[2,1,8,1]{0,3,1,2:T(1,128)}), f32[2,1,8,1]{0,3,1,2:T(1,128)S(1)}, u32[]{:S(2)}, u32[]{:S(2)}) async-start(f32[2,1,8,1]{0,3,1,2:T(1,128)} %broadcast_in_dim.8), calls=%async_computation | async-start | bytes 8192 | tf_op jit(solution)/shard_map/all_to_all | solution.py:82
  18.7 0.1 fusion.17
  18.8 0.7 %divide_bitcast_fusion = f32[2,128]{1,0:T(2,128)S(1)} fusion(f32[256]{0:T(256)S(1)} %fusion.17, f32[]{:T(128)} %get-tuple-element.105), kind=kLoop, calls=%fused_computation.48 | loop fusion | flops 256 | bytes 2052 | tf_op jit(solution)/shard_map/div | solution.py:19
  19.5 0.2 fusion.21
  19.7 9.3 %while.13 = (s32[]{:T(128)}, f32[2,72,128]{2,1,0:T(8,128)S(1)}, f32[8,2]{1,0:T(8,128)S(1)}, s32[8,32,128]{2,1,0:T(8,128)S(1)}, bf16[8,32,128]{2,1,0:T(8,128)(2,1...) while((s32[]{:T(128)}, f32[2,72,128]{2,1,0:T(8,128)S(1)}, f32[8,2]{1,0:T(8,128)S(1)}, ...), condition=%wide.region_4.5_spmd.clone, body=%wide.region_3.4_spmd.clone.sunk | while | flops 78440448 | bytes 1548619 | solution.py:70
  19.8 0.1 fusion.35
  20.0 0.8 %fusion.36 = f32[72,128]{1,0:T(8,128)S(1)} fusion(s32[32,128]{1,0:T(8,128)S(1)} %add_select_fusion.5, bf16[32,128,24]{1,2,0:T(8,128)(2,1)S(1)} %fusion.33, bf16[32,128,24]{1,2,0:T(8,128)(2,1)S(1)} %get-tuple-element.169, bf16[32,128,24]{1,2,0:T(8,128)(2,1)S(1)} %get-tuple-element.170), kind=kOutput, calls=%fused_computation.2.clone.1 | convolution fusion | flops 77791232 | bytes 643072 | tf_op jit(solution)/shard_map/while/body/eval_jaxpr/dot_general | solution.py:64
  20.8 0.1 select_add_fusion.2
  21.0 0.1 fusion.35
  21.2 0.8 %fusion.36 = f32[72,128]{1,0:T(8,128)S(1)} fusion(s32[32,128]{1,0:T(8,128)S(1)} %add_select_fusion.5, bf16[32,128,24]{1,2,0:T(8,128)(2,1)S(1)} %fusion.33, bf16[32,128,24]{1,2,0:T(8,128)(2,1)S(1)} %get-tuple-element.169, bf16[32,128,24]{1,2,0:T(8,128)(2,1)S(1)} %get-tuple-element.170), kind=kOutput, calls=%fused_computation.2.clone.1 | convolution fusion | flops 77791232 | bytes 643072 | tf_op jit(solution)/shard_map/while/body/eval_jaxpr/dot_general | solution.py:64
  22.0 0.1 select_add_fusion.2
  22.1 0.1 fusion.35
  22.3 0.8 %fusion.36 = f32[72,128]{1,0:T(8,128)S(1)} fusion(s32[32,128]{1,0:T(8,128)S(1)} %add_select_fusion.5, bf16[32,128,24]{1,2,0:T(8,128)(2,1)S(1)} %fusion.33, bf16[32,128,24]{1,2,0:T(8,128)(2,1)S(1)} %get-tuple-element.169, bf16[32,128,24]{1,2,0:T(8,128)(2,1)S(1)} %get-tuple-element.170), kind=kOutput, calls=%fused_computation.2.clone.1 | convolution fusion | flops 77791232 | bytes 643072 | tf_op jit(solution)/shard_map/while/body/eval_jaxpr/dot_general | solution.py:64
  23.1 0.1 select_add_fusion.2
  23.3 0.1 fusion.35
  23.5 0.8 %fusion.36 = f32[72,128]{1,0:T(8,128)S(1)} fusion(s32[32,128]{1,0:T(8,128)S(1)} %add_select_fusion.5, bf16[32,128,24]{1,2,0:T(8,128)(2,1)S(1)} %fusion.33, bf16[32,128,24]{1,2,0:T(8,128)(2,1)S(1)} %get-tuple-element.169, bf16[32,128,24]{1,2,0:T(8,128)(2,1)S(1)} %get-tuple-element.170), kind=kOutput, calls=%fused_computation.2.clone.1 | convolution fusion | flops 77791232 | bytes 643072 | tf_op jit(solution)/shard_map/while/body/eval_jaxpr/dot_general | solution.py:64
  24.3 0.1 select_add_fusion.2
  24.4 0.1 fusion.35
  24.6 0.8 %fusion.36 = f32[72,128]{1,0:T(8,128)S(1)} fusion(s32[32,128]{1,0:T(8,128)S(1)} %add_select_fusion.5, bf16[32,128,24]{1,2,0:T(8,128)(2,1)S(1)} %fusion.33, bf16[32,128,24]{1,2,0:T(8,128)(2,1)S(1)} %get-tuple-element.169, bf16[32,128,24]{1,2,0:T(8,128)(2,1)S(1)} %get-tuple-element.170), kind=kOutput, calls=%fused_computation.2.clone.1 | convolution fusion | flops 77791232 | bytes 643072 | tf_op jit(solution)/shard_map/while/body/eval_jaxpr/dot_general | solution.py:64
  25.5 0.1 select_add_fusion.2
  25.6 0.1 fusion.35
  25.8 0.8 %fusion.36 = f32[72,128]{1,0:T(8,128)S(1)} fusion(s32[32,128]{1,0:T(8,128)S(1)} %add_select_fusion.5, bf16[32,128,24]{1,2,0:T(8,128)(2,1)S(1)} %fusion.33, bf16[32,128,24]{1,2,0:T(8,128)(2,1)S(1)} %get-tuple-element.169, bf16[32,128,24]{1,2,0:T(8,128)(2,1)S(1)} %get-tuple-element.170), kind=kOutput, calls=%fused_computation.2.clone.1 | convolution fusion | flops 77791232 | bytes 643072 | tf_op jit(solution)/shard_map/while/body/eval_jaxpr/dot_general | solution.py:64
  26.6 0.1 select_add_fusion.2
  26.7 0.1 fusion.35
  26.9 0.8 %fusion.36 = f32[72,128]{1,0:T(8,128)S(1)} fusion(s32[32,128]{1,0:T(8,128)S(1)} %add_select_fusion.5, bf16[32,128,24]{1,2,0:T(8,128)(2,1)S(1)} %fusion.33, bf16[32,128,24]{1,2,0:T(8,128)(2,1)S(1)} %get-tuple-element.169, bf16[32,128,24]{1,2,0:T(8,128)(2,1)S(1)} %get-tuple-element.170), kind=kOutput, calls=%fused_computation.2.clone.1 | convolution fusion | flops 77791232 | bytes 643072 | tf_op jit(solution)/shard_map/while/body/eval_jaxpr/dot_general | solution.py:64
  27.8 0.1 select_add_fusion.2
  27.9 0.1 fusion.35
  28.1 0.8 %fusion.36 = f32[72,128]{1,0:T(8,128)S(1)} fusion(s32[32,128]{1,0:T(8,128)S(1)} %add_select_fusion.5, bf16[32,128,24]{1,2,0:T(8,128)(2,1)S(1)} %fusion.33, bf16[32,128,24]{1,2,0:T(8,128)(2,1)S(1)} %get-tuple-element.169, bf16[32,128,24]{1,2,0:T(8,128)(2,1)S(1)} %get-tuple-element.170), kind=kOutput, calls=%fused_computation.2.clone.1 | convolution fusion | flops 77791232 | bytes 643072 | tf_op jit(solution)/shard_map/while/body/eval_jaxpr/dot_general | solution.py:64
  28.9 0.1 select_add_fusion.2
  29.0 0.7 %copy.37 = f32[2,3,8,384]{3,0,1,2:T(2,128)} copy(f32[2,3,8,384]{3,2,1,0:T(8,128)S(1)} %reshape_reshape.3) | data formatting | bytes 147456 | tf_op jit(solution)/shard_map/reshape;reshape | solution.py:76
  29.7 5.0 %all-to-all-start.2 = ((f32[2,3,8,384]{3,0,1,2:T(2,128)}), f32[2,3,8,384]{3,0,1,2:T(2,128)S(1)}, u32[]{:S(2)}, u32[]{:S(2)}) async-start(f32[2,3,8,384]{3,0,1,2:T(2,128)} %copy.37), calls=%async_computation.2 | async-start | bytes 147456 | tf_op jit(solution)/shard_map/all_to_all | solution.py:81
  34.7 0.6 %dynamic-slice = u32[1]{0:T(128)} dynamic-slice(u32[32]{0:T(128)S(1)} %copy-done.4, u32[]{:T(128)S(6)} %add.43), dynamic_slice_sizes={1} | dynamic-slice | bytes 12
  36.0 0.1 copy.32
  36.0 0.1 copy.33
  36.1 0.1 eq.87
  36.2 4.5 %all-to-all-done.2 = f32[2,3,8,384]{3,0,1,2:T(2,128)S(1)} async-done(((f32[2,3,8,384]{3,0,1,2:T(2,128)}), f32[2,3,8,384]{3,0,1,2:T(2,128)S(1)}, u32[]{:S(2)}, u32[]{:S(2)}) %all-to-all-start.2) | async-done | bytes 73760 | tf_op jit(solution)/shard_map/all_to_all | solution.py:81
  40.7 0.1 fusion.18
  40.9 8.6 %all-reduce = f32[8,3,384]{2,0,1:T(8,128)S(1)} all-reduce(f32[8,3,384]{2,0,1:T(8,128)S(1)} %fusion.18), channel_id=2, replica_groups=mesh['groups'=2,'det'=4,'blk'=2,'sub'=2] {'blk'}, use_global_device_ids=true, to_apply=%region_5.6.clone | all-reduce | flops 9216 | bytes 73728
  49.5 0.6 %dynamic-slice_bitcast_fusion.1 = (f32[4,384]{1,0:T(4,128)}, f32[4,384]{1,0:T(4,128)}, f32[4,384]{1,0:T(4,128)}) fusion(f32[8,3,384]{2,0,1:T(8,128)S(1)} %all-reduce, u32[]{:T(128)S(6)} %multiply.1, u32[]{:T(128)S(6)} %convert.1, u32[]{:T(128)S(6)} %convert), kind=kLoop, calls=%fused_computation.37 | loop fusion | bytes 36876 | tf_op jit(solution)/shard_map/squeeze | solution.py:98
  (68 shorter events, 1.1 us)
Async XLA Ops:
  2.2 6.5 %copy-start.2 = (f32[8]{0:T(128)S(1)}, f32[8]{0:T(128)}, u32[]{:S(2)}) copy-start(f32[8]{0:T(128)} %param.11) | copy-start | bytes 100
  2.2 6.5 %copy-start.3 = (s32[128]{0:T(128)S(1)}, s32[128]{0:T(128)}, u32[]{:S(2)}) copy-start(s32[128]{0:T(128)} %param.10) | copy-start | bytes 1540
  2.2 7.3 %copy-start = (s32[128,1,256]{2,1,0:T(1,128)S(1)}, s32[128,1,256]{2,1,0:T(1,128)}, u32[]{:S(2)}) copy-start(s32[128,1,256]{2,1,0:T(1,128)} %param.8) | copy-start | bytes 393220
  2.2 12.6 %all-to-all-start.1 = ((f32[32,4,256]{2,0,1:T(8,128)}), f32[32,4,256]{2,0,1:T(8,128)S(1)}, u32[]{:S(2)}, u32[]{:S(2)}) async-start(f32[32,4,256]{2,0,1:T(8,128)} %copy.35), calls=%async_computation.1 | async-start | bytes 262144 | tf_op jit(solution)/shard_map/all_to_all | solution.py:18
  8.7 0.9 %copy-start.1 = (s32[4,2]{0,1:T(2,128)S(1)}, s32[4,2]{0,1:T(2,128)}, u32[]{:S(2)}) copy-start(s32[4,2]{0,1:T(2,128)} %param.9) | copy-start | bytes 100
  15.3 14.3 %all-to-all-start = ((f32[2,1,8,1]{0,3,1,2:T(1,128)}), f32[2,1,8,1]{0,3,1,2:T(1,128)S(1)}, u32[]{:S(2)}, u32[]{:S(2)}) async-start(f32[2,1,8,1]{0,3,1,2:T(1,128)} %broadcast_in_dim.8), calls=%async_computation | async-start | bytes 8192 | tf_op jit(solution)/shard_map/all_to_all | solution.py:82
  29.0 5.7 %copy-start.4 = (u32[32]{0:T(128)S(1)}, u32[32]{0:T(128)}, u32[]{:S(2)}) copy-start(u32[32]{0:T(128)} %constant.84) | copy-start | bytes 388
  29.7 11.0 %all-to-all-start.2 = ((f32[2,3,8,384]{3,0,1,2:T(2,128)}), f32[2,3,8,384]{3,0,1,2:T(2,128)S(1)}, u32[]{:S(2)}, u32[]{:S(2)}) async-start(f32[2,3,8,384]{3,0,1,2:T(2,128)} %copy.37), calls=%async_computation.2 | async-start | bytes 147456 | tf_op jit(solution)/shard_map/all_to_all | solution.py:81
where the time goes:
time: 50.5 us; the launch traced here: 50.1 us
  starting transfers between devices  14.8 us (29%)
  waiting for transfers between devices  9.42 us (19%)
  blocking collectives  8.57 us (17%)
  matrix products  6.57 us (13%)
  local copies, waits for them, and re-layouts  4.85 us (10%)
  other arithmetic  4.02 us (8%)
  between operations  1.39 us (3%)
    unnamed x1, blocking collectives  8.57 us
    all_to_all x1, starting transfers between devices, on_device(): lax.all_to_all(tod, 'det', split_axis=1, concat_axis=0, tiled=True)  6.48 us
    dot_general x8, matrix products, bin_tile(): lax.dot_general(stacked, low_hot, (((0,), (0,)), ((), ())), preferred_ele...  6.42 us
    all_to_all x1, starting transfers between devices, on_device(): lax.all_to_all(pieces, ('det', 'sub'), split_axis=2, concat_axis=0, tiled...  5.03 us
    all_to_all x1, waiting for transfers between devices, on_device(): lax.all_to_all(tod, 'det', split_axis=1, concat_axis=0, tiled=True)  4.93 us
    all_to_all x1, waiting for transfers between devices, on_device(): lax.all_to_all(pieces, ('det', 'sub'), split_axis=2, concat_axis=0, tiled...  4.49 us
    all_to_all x1, starting transfers between devices, on_device(): lax.all_to_all(labels, ('det', 'sub'), split_axis=2, concat_axis=0, tiled...  3.31 us
    unnamed x12, local copies, waits for them, and re-layouts  2.17 us
  transfers between devices with their start and end apart: 3, of which 2 were waited for; matrix products, arithmetic and copies ran while one was open for 25% of the time, Pallas kernels for 0%

commit v1 on v0

v1 whole, which is shorter than its diff:
```python
import functools

import jax
import jax.numpy as jnp
from jax import lax
from jax.experimental import pallas as pl
from jax.experimental.pallas import tpu as pltpu
from jax.sharding import PartitionSpec as P

BLOCK_PIX = 3072
SPAN = 128
BLK_OWN = 4
VMEM = pltpu.MemorySpace.VMEM
SMEM = pltpu.MemorySpace.SMEM


def partner(index, step, count):
    return index ^ step if count & (count - 1) == 0 else lax.rem(index + step, count)


def source(index, step, count):
    return index ^ step if count & (count - 1) == 0 else lax.rem(index + count - step, count)


def exchange(x, axes, step, count):
    power = count & (count - 1) == 0
    pairs = [(i, i ^ step if power else (i + step) % count) for i in range(count)]
    return lax.ppermute(x, axes, pairs)


def call(kernel, outs, ins, scratch=(), limit=16 << 20, flops=1 << 20, moved=1 << 20):
    return pl.pallas_call(
        kernel,
        out_shape=outs,
        in_specs=[pl.BlockSpec(memory_space=space) for space in ins],
        out_specs=[pl.BlockSpec(memory_space=VMEM) for _ in outs],
        scratch_shapes=list(scratch),
        compiler_params=pltpu.CompilerParams(vmem_limit_bytes=limit),
        cost_estimate=pl.CostEstimate(flops=flops, bytes_accessed=moved, transcendentals=0),
    )


def cut_kernel(count, tod_ref, *outs):
    me = lax.axis_index("det")
    for step, out in enumerate(outs):
        segment = partner(me, step, count)
        for d in range(tod_ref.shape[0]):
            out[pl.ds(d, 1), :] = tod_ref[d, pl.ds(segment, 1), :]


def bin_kernel(count, lanes, upper, pad, rows, group, pix_ref, weight_ref, *refs):
    parts, outs = refs[:count], refs[count : 2 * count]
    value_ref, low_ref, high_ref, scale_ref, total_ref = refs[2 * count :]
    me = lax.axis_index("det")
    held, samples = parts[0].shape
    spans = samples // SPAN
    weight_all = jnp.sum(weight_ref[...], axis=0, keepdims=True)
    common = [jnp.zeros((1, SPAN), jnp.float32) for _ in range(spans)]
    for step in range(count):
        first = pl.multiple_of(source(me, step, count) * held, held)
        weight = weight_ref[pl.ds(first, held), :]
        scale_ref[0, step * held : (step + 1) * held, :] = weight
        for c in range(spans):
            common[c] += jnp.sum(
                weight * parts[step][:, c * SPAN : (c + 1) * SPAN], axis=0, keepdims=True
            )
        for c in range(spans):
            pix = pix_ref[pl.ds(first, held), c * SPAN : (c + 1) * SPAN]
            high = ((pix.astype(jnp.float32) + 0.5) * (1.0 / lanes)).astype(jnp.int32)
            low = pix - high * lanes
            high_ref[c, step * held : (step + 1) * held, :] = high.astype(jnp.float32)
            low_ref[c, step * held : (step + 1) * held, :] = low.astype(jnp.float32)
    for step in range(count):
        weight = scale_ref[0, step * held : (step + 1) * held, :]
        for c in range(spans):
            value_ref[c, step * held : (step + 1) * held, :] = weight * (
                parts[step][:, c * SPAN : (c + 1) * SPAN] - common[c] / weight_all
            )

    tile = 16

    def spread(ref, d, c):
        return ref[c, pl.ds(d, tile, stride=0), :].astype(jnp.bfloat16)

    number = lax.broadcasted_iota(jnp.int32, (tile, SPAN), 0).astype(jnp.float32)
    low_number = [(number + i).astype(jnp.bfloat16) for i in range(0, lanes, tile)]
    one = jnp.ones((tile, SPAN), jnp.bfloat16)
    zero = jnp.zeros((tile, SPAN), jnp.bfloat16)
    for c in range(spans):

        def step(g, acc):
            left, right = [], []
            for u in range(group):
                d = g * group + u
                low = spread(low_ref, d, c)
                high = spread(high_ref, d, c)
                value = spread(value_ref, d, c)
                scale = spread(scale_ref, d, 0)
                right.append(
                    jnp.concatenate([jnp.where(low == n, one, zero) for n in low_number], axis=0)
                )
                hot = [high == n for n in low_number[: pad // tile]]
                left.append(
                    jnp.concatenate(
                        [jnp.where(h, x, zero) for x in (value, scale, one) for h in hot], axis=0
                    )
                )
            return acc + lax.dot_general(
                jnp.concatenate(left, axis=1),
                jnp.concatenate(right, axis=1),
                (((1,), (1,)), ((), ())),
                preferred_element_type=jnp.float32,
            )

        total_ref[c] = lax.fori_loop(
            0, count * held // group, step, jnp.zeros((3 * pad, lanes), jnp.float32)
        )
    for step in range(count):
        first = partner(me, step, count) * rows
        for c in range(spans):
            for q in range(3):
                at = (c * 3 + q) * rows
                outs[step][at : at + rows, :] = total_ref[c, pl.ds(q * pad + first, rows), :]


def place_kernel(count, blks, subs, spans, own, label_ref, *refs):
    parts, outs = refs[:count], refs[count:]
    me = lax.axis_index("det")
    lanes = parts[0].shape[1]
    here = lax.axis_index("blk") * subs + lax.axis_index("sub")
    for step, out in enumerate(outs):
        to = partner(here, step, blks * subs)
        block, sub = to // subs, lax.rem(to, subs)
        number = lax.broadcasted_iota(jnp.int32, (BLK_OWN, lanes), 0) + block * BLK_OWN
        masks = [
            [number == label_ref[source(me, k, count) * spans + c] for c in range(spans)]
            for k in range(count)
        ]
        for q in range(3):
            for r in range(own):
                total = jnp.zeros((BLK_OWN, lanes), jnp.float32)
                for k in range(count):
                    for c in range(spans):
                        row = (c * 3 + q) * subs * own + sub * own + r
                        part = parts[k][pl.ds(row, BLK_OWN, stride=0), :]
                        total += jnp.where(masks[k][c], part, 0.0)
                at = (q * own + r) * BLK_OWN
                out[at : at + BLK_OWN, :] = total


def on_device(tod, pixels, span_block, weight_class, class_weight):
    dets, blks, subs = (lax.axis_size(name) for name in ("det", "blk", "sub"))
    held, _, samples = tod.shape
    detectors = pixels.shape[0]
    spans = samples // SPAN
    width = BLOCK_PIX // (dets * subs)
    lanes = max(n for n in range(1, 129) if width % n == 0)
    own = width // lanes
    upper = BLOCK_PIX // lanes
    pad = -(-upper // 16) * 16
    f32 = jnp.float32

    cut = call(
        functools.partial(cut_kernel, dets),
        [jax.ShapeDtypeStruct((held, samples), f32)] * dets,
        [VMEM],
    )(tod)
    parts = [cut[0]] + [exchange(cut[k], "det", k, dets) for k in range(1, dets)]

    classes = jnp.arange(class_weight.shape[0], dtype=jnp.int32)
    picker = (weight_class[:, None] == classes[None, :]).astype(f32)
    weight = jnp.sum(picker * class_weight[None, :], axis=1)
    weight = jnp.broadcast_to(weight[:, None], (detectors, SPAN))

    rows = subs * own
    shape = jax.ShapeDtypeStruct((spans * 3 * rows, lanes), f32)
    chunks = call(
        functools.partial(bin_kernel, dets, lanes, upper, pad, rows, 4),
        [shape] * dets,
        [VMEM] * (2 + dets),
        [
            pltpu.VMEM((spans, detectors, SPAN), f32),
            pltpu.VMEM((spans, detectors, SPAN), f32),
            pltpu.VMEM((spans, detectors, SPAN), f32),
            pltpu.VMEM((1, detectors, SPAN), f32),
            pltpu.VMEM((spans, 3 * pad, lanes), f32),
        ],
    )(pixels.reshape(detectors, samples), weight, *parts)
    chunks = [chunks[0]] + [exchange(chunks[k], "det", k, dets) for k in range(1, dets)]

    peers = blks * subs
    shape = jax.ShapeDtypeStruct((3 * own * BLK_OWN, lanes), f32)
    placed = call(
        functools.partial(place_kernel, dets, blks, subs, spans, own),
        [shape] * peers,
        [SMEM] + [VMEM] * dets,
    )(span_block.reshape(-1), *chunks)
    total = placed[0]
    for k in range(1, peers):
        total = total + exchange(placed[k], ("blk", "sub"), k, peers)
    total = total.reshape(3, own, BLK_OWN, lanes).transpose(0, 2, 1, 3)
    total = total.reshape(3, BLK_OWN, width)
    return total[0], total[1], total[2]


def solution(mesh):
    placed = (
        P(("groups", "det"), None, ("blk", "sub")),
        P("groups", "det", ("blk", "sub")),
        P("groups", ("blk", "sub")),
        P("groups"),
        P("groups"),
    )
    return jax.shard_map(
        on_device,
        mesh=mesh,
        in_specs=placed,
        out_specs=(P(("groups", "blk"), ("det", "sub")),) * 3,
        check_vma=False,
    )
```

time: 50.5 us -> 38 us (0.75)
  Pallas kernels: 0 us -> 12.7 us
  blocking collectives: 8.57 us -> 0 us
  matrix products: 6.57 us -> 0 us
  other arithmetic: 4.02 us -> 0.09 us
  local copies, waits for them, and re-layouts: 4.85 us -> 1.79 us
  starting transfers between devices: 14.8 us -> 12.1 us
  waiting for transfers between devices: 9.42 us -> 10.4 us
  between operations: 1.39 us -> 0.72 us
    all_to_all x3 -> x0, starting transfers between devices: 14.8 us -> none  [the longest x1 6.48 us: on_device(): lax.all_to_all(tod, 'det', split_axis=1, concat_axis=0, tiled=True)]
    pallas_call x0 -> x3, Pallas kernels: none -> 12.7 us  [the longest x1 12 us: on_device(): call(functools.partial(bin_kernel, dets, lanes, upper, pad, rows, 4), [sh...]
    ppermute x0 -> x9, starting transfers between devices: none -> 12.1 us  [exchange(): return lax.ppermute(x, axes, pairs)]
    ppermute x0 -> x9, waiting for transfers between devices: none -> 10.4 us  [exchange(): return lax.ppermute(x, axes, pairs)]
    all_to_all x3 -> x0, waiting for transfers between devices: 9.42 us -> none  [the longest x1 4.93 us: on_device(): lax.all_to_all(tod, 'det', split_axis=1, concat_axis=0, tiled=True)]
    unnamed x1 -> x0, blocking collectives: 8.57 us -> none
    dot_general x9 -> x0, matrix products: 6.57 us -> none  [the longest x8 6.42 us: bin_tile(): lax.dot_general(stacked, low_hot, (((0,), (0,)), ((), ())), preferred_ele...]
    unnamed x12, local copies, waits for them, and re-layouts: 2.17 us -> 1.02 us
  transfers between devices with their start and end apart: 3 -> 9, of which waited for: 2 -> 6; matrix products, arithmetic and copies ran while one was open for 25% -> 1% of each run, Pallas kernels for 0% -> 0%
where the time goes in v1:
time: 38 us; the launch traced here: 37.8 us
  Pallas kernels  12.7 us (33%)
  starting transfers between devices  12.1 us (32%)
  waiting for transfers between devices  10.4 us (27%)
  local copies, waits for them, and re-layouts  1.79 us (5%)
  between operations  0.72 us (2%)
    ppermute x9, starting transfers between devices, exchange(): return lax.ppermute(x, axes, pairs)  12.1 us
    pallas_call x1, Pallas kernels, on_device(): call(functools.partial(bin_kernel, dets, lanes, upper, pad, rows, 4), [sh...  12 us
    ppermute x9, waiting for transfers between devices, exchange(): return lax.ppermute(x, axes, pairs)  10.4 us
    unnamed x12, local copies, waits for them, and re-layouts  1.02 us
  transfers between devices with their start and end apart: 9, of which 6 were waited for; matrix products, arithmetic and copies ran while one was open for 1% of the time, Pallas kernels for 0%

profile of v1, /device:TPU:0, one launch (start us, length us, event | category | flops | bytes accessed | tf_op | source)
XLA Modules:
  0.0 37.8 jit_solution(18026486081203366691)
XLA Ops:
  0.6 0.0 copy-start
  0.6 0.9 %copy-done = f32[32,4,256]{2,1,0:T(4,128)S(1)} copy-done((f32[32,4,256]{2,1,0:T(4,128)S(1)}, f32[32,4,256]{2,1,0:T(4,128)}, u32[]{:S(2)}) %copy-start) | copy-done | bytes 131096
  1.5 0.0 copy-start.1
  1.5 0.1 shard_map.76
  1.6 3.1 %collective-permute-start = (f32[32,256]{1,0:T(8,128)S(1)}, f32[32,256]{1,0:T(8,128)S(1)}, u32[]{:S(2)}, u32[]{:S(2)}) collective-permute-start(f32[32,256]{1,0:T(8,128)S(1)} %get-tuple-element.16), channel_id=1, source_target_pairs={{0,4},{4,0},{8,12},{12,8},{1,5},{5,1},{9,13},{13,9},{2,6},{6,2},{1... | collective-permute-start | bytes 98312 | tf_op jit(solution)/shard_map/ppermute | solution.py:28
  4.7 0.0 copy-start.3
  4.7 0.0 copy-start.4
  4.7 2.6 %collective-permute-start.1 = (f32[32,256]{1,0:T(8,128)S(1)}, f32[32,256]{1,0:T(8,128)S(1)}, u32[]{:S(2)}, u32[]{:S(2)}) collective-permute-start(f32[32,256]{1,0:T(8,128)S(1)} %get-tuple-element.17), channel_id=1, source_target_pairs={{0,8},{4,12},{8,0},{12,4},{1,9},{5,13},{9,1},{13,5},{2,10},{6,14},... | collective-permute-start | bytes 98312 | tf_op jit(solution)/shard_map/ppermute | solution.py:28
  7.3 0.0 collective-permute-start.2
  7.3 0.0 copy-done.3
  7.3 0.0 copy-done.4
  7.3 0.1 select_reduce_fusion
  7.4 0.0 copy-done.1
  7.4 0.0 collective-permute-done.refs_1_
  7.4 2.7 %collective-permute-done.1.refs_2_ = f32[32,256]{1,0:T(8,128)S(1)} collective-permute-done((f32[32,256]{1,0:T(8,128)S(1)}, f32[32,256]{1,0:T(8,128)S(1)}, u32[]{:S(2)}, u32[]{:S(2)}) %collective-permute-start.1) | collective-permute-done | bytes 32800 | tf_op jit(solution)/shard_map/ppermute | solution.py:28
  10.1 2.9 %collective-permute-done.2.refs_3_ = f32[32,256]{1,0:T(8,128)S(1)} collective-permute-done((f32[32,256]{1,0:T(8,128)S(1)}, f32[32,256]{1,0:T(8,128)S(1)}, u32[]{:S(2)}, u32[]{:S(2)}) %collective-permute-start.2) | collective-permute-done | bytes 32800 | tf_op jit(solution)/shard_map/ppermute | solution.py:28
  13.0 0.1 broadcast_in_dim.2.weight_ref
  13.1 12.0 %shard_map.77 = (f32[36,128]{1,0:T(8,128)S(1)}, f32[36,128]{1,0:T(8,128)S(1)}, f32[36,128]{1,0:T(8,128)S(1)}, f32[36,128]{1,0:T(8,128)S(1)}) custom-call(s32[128,256]{1,0:T(8,128)S(1)} %bitcast.10, f32[128,128]{1,0:T(8,128)S(1)} %broadcast_in_dim.2.weight_ref, f32[32,256]{1,0:T(8,128)S(1)} %get-tuple-element.15.refs_0_, ...), custom_call_target="tpu_custom_call" | custom-call | flops 1048576 | bytes 1048576 | tf_op jit(solution)/shard_map/pallas_call | solution.py:177
  25.1 0.1 collective-permute-start.3
  25.2 0.0 copy-start.2
  25.2 0.9 %collective-permute-start.4 = (f32[36,128]{1,0:T(8,128)S(1)}, f32[36,128]{1,0:T(8,128)S(1)}, u32[]{:S(2)}, u32[]{:S(2)}) collective-permute-start(f32[36,128]{1,0:T(8,128)S(1)} %get-tuple-element.21), channel_id=1, source_target_pairs={{0,8},{4,12},{8,0},{12,4},{1,9},{5,13},{9,1},{13,5},{2,10},{6,14},... | collective-permute-start | bytes 55304 | tf_op jit(solution)/shard_map/ppermute | solution.py:28
  26.1 3.5 %collective-permute-start.5 = (f32[36,128]{1,0:T(8,128)S(1)}, f32[36,128]{1,0:T(8,128)S(1)}, u32[]{:S(2)}, u32[]{:S(2)}) collective-permute-start(f32[36,128]{1,0:T(8,128)S(1)} %get-tuple-element.22), channel_id=1, source_target_pairs={{0,12},{4,8},{8,4},{12,0},{1,13},{5,9},{9,5},{13,1},{2,14},{6,10},... | collective-permute-start | bytes 55304 | tf_op jit(solution)/shard_map/ppermute | solution.py:28
  29.5 0.0 copy-done.2
  29.5 0.1 copy.13
  29.6 0.1 reshape.25.label_ref
  29.7 0.0 collective-permute-done.3.refs_1_
  29.7 0.2 collective-permute-done.4.refs_2_
  29.9 1.7 %collective-permute-done.5.refs_3_ = f32[36,128]{1,0:T(8,128)S(1)} collective-permute-done((f32[36,128]{1,0:T(8,128)S(1)}, f32[36,128]{1,0:T(8,128)S(1)}, u32[]{:S(2)}, u32[]{:S(2)}) %collective-permute-start.5) | collective-permute-done | bytes 18464 | tf_op jit(solution)/shard_map/ppermute | solution.py:28
  31.6 0.7 %shard_map.78 = (f32[36,128]{1,0:T(8,128)S(1)}, f32[36,128]{1,0:T(8,128)S(1)}, f32[36,128]{1,0:T(8,128)S(1)}, f32[36,128]{1,0:T(8,128)S(1)}) custom-call(s32[8]{0:T(128)S(1)} %reshape.25.label_ref, f32[36,128]{1,0:T(8,128)S(1)} %get-tuple-element.19.refs_0_, f32[36,128]{1,0:T(8,128)S(1)} %collective-permute-done.3.refs_1_, ...), custom_call_target="tpu_custom_call" | custom-call | flops 1048576 | bytes 1048576 | tf_op jit(solution)/shard_map/pallas_call | solution.py:193
  32.4 0.1 collective-permute-start.6
  32.4 1.6 %collective-permute-start.7 = (f32[36,128]{1,0:T(8,128)S(1)}, f32[36,128]{1,0:T(8,128)S(1)}, u32[]{:S(2)}, u32[]{:S(2)}) collective-permute-start(f32[36,128]{1,0:T(8,128)S(1)} %get-tuple-element.25), channel_id=1, source_target_pairs={{0,2},{1,3},{2,0},{3,1},{4,6},{5,7},{6,4},{7,5},{8,10},{9,11},{10,... | collective-permute-start | bytes 55304 | tf_op jit(solution)/shard_map/ppermute | solution.py:28
  34.0 0.3 collective-permute-start.8
  34.3 0.0 collective-permute-done.6
  34.3 2.0 %collective-permute-done.7 = f32[36,128]{1,0:T(8,128)S(1)} collective-permute-done((f32[36,128]{1,0:T(8,128)S(1)}, f32[36,128]{1,0:T(8,128)S(1)}, u32[]{:S(2)}, u32[]{:S(2)}) %collective-permute-start.7) | collective-permute-done | bytes 18464 | tf_op jit(solution)/shard_map/ppermute | solution.py:28
  36.3 0.9 %collective-permute-done.8 = f32[36,128]{1,0:T(8,128)S(1)} collective-permute-done((f32[36,128]{1,0:T(8,128)S(1)}, f32[36,128]{1,0:T(8,128)S(1)}, u32[]{:S(2)}, u32[]{:S(2)}) %collective-permute-start.8) | collective-permute-done | bytes 18464 | tf_op jit(solution)/shard_map/ppermute | solution.py:28
  37.2 0.6 %slice_bitcast_fusion = (f32[4,384]{1,0:T(4,128)}, f32[4,384]{1,0:T(4,128)}, f32[4,384]{1,0:T(4,128)}) fusion(f32[3,4,3,128]{3,1,2,0:T(4,128)S(1)} %bitcast.11), kind=kLoop, calls=%fused_computation.2 | loop fusion | bytes 36864 | tf_op jit(solution)/shard_map/squeeze | solution.py:203
  (3 shorter events, 0.0 us)
Async XLA Ops:
  0.6 0.9 %copy-start = (f32[32,4,256]{2,1,0:T(4,128)S(1)}, f32[32,4,256]{2,1,0:T(4,128)}, u32[]{:S(2)}) copy-start(f32[32,4,256]{2,1,0:T(4,128)} %tod_ref.1) | copy-start | bytes 393220
  1.5 5.9 %copy-start.1 = (s32[128,1,256]{2,1,0:T(1,128)S(1)}, s32[128,1,256]{2,1,0:T(1,128)}, u32[]{:S(2)}) copy-start(s32[128,1,256]{2,1,0:T(1,128)} %param.6) | copy-start | bytes 393220
  1.6 5.8 %collective-permute-start = (f32[32,256]{1,0:T(8,128)S(1)}, f32[32,256]{1,0:T(8,128)S(1)}, u32[]{:S(2)}, u32[]{:S(2)}) collective-permute-start(f32[32,256]{1,0:T(8,128)S(1)} %get-tuple-element.16), channel_id=1, source_target_pairs={{0,4},{4,0},{8,12},{12,8},{1,5},{5,1},{9,13},{13,9},{2,6},{6,2},{1... | collective-permute-start | bytes 98312 | tf_op jit(solution)/shard_map/ppermute | solution.py:28
  4.7 2.6 %copy-start.3 = (f32[8]{0:T(128)S(1)}, f32[8]{0:T(128)}, u32[]{:S(2)}) copy-start(f32[8]{0:T(128)} %param.9) | copy-start | bytes 100
  4.7 2.6 %copy-start.4 = (s32[128]{0:T(128)S(1)}, s32[128]{0:T(128)}, u32[]{:S(2)}) copy-start(s32[128]{0:T(128)} %param.8) | copy-start | bytes 1540
  4.7 5.4 %collective-permute-start.1 = (f32[32,256]{1,0:T(8,128)S(1)}, f32[32,256]{1,0:T(8,128)S(1)}, u32[]{:S(2)}, u32[]{:S(2)}) collective-permute-start(f32[32,256]{1,0:T(8,128)S(1)} %get-tuple-element.17), channel_id=1, source_target_pairs={{0,8},{4,12},{8,0},{12,4},{1,9},{5,13},{9,1},{13,5},{2,10},{6,14},... | collective-permute-start | bytes 98312 | tf_op jit(solution)/shard_map/ppermute | solution.py:28
  7.3 5.7 %collective-permute-start.2 = (f32[32,256]{1,0:T(8,128)S(1)}, f32[32,256]{1,0:T(8,128)S(1)}, u32[]{:S(2)}, u32[]{:S(2)}) collective-permute-start(f32[32,256]{1,0:T(8,128)S(1)} %get-tuple-element.18), channel_id=1, source_target_pairs={{0,12},{4,8},{8,4},{12,0},{1,13},{5,9},{9,5},{13,1},{2,14},{6,10},... | collective-permute-start | bytes 98312 | tf_op jit(solution)/shard_map/ppermute | solution.py:28
  25.1 4.6 %collective-permute-start.3 = (f32[36,128]{1,0:T(8,128)S(1)}, f32[36,128]{1,0:T(8,128)S(1)}, u32[]{:S(2)}, u32[]{:S(2)}) collective-permute-start(f32[36,128]{1,0:T(8,128)S(1)} %get-tuple-element.20), channel_id=1, source_target_pairs={{0,4},{4,0},{8,12},{12,8},{1,5},{5,1},{9,13},{13,9},{2,6},{6,2},{1... | collective-permute-start | bytes 55304 | tf_op jit(solution)/shard_map/ppermute | solution.py:28
  25.2 4.4 %copy-start.2 = (s32[4,2]{0,1:T(2,128)S(1)}, s32[4,2]{0,1:T(2,128)}, u32[]{:S(2)}) copy-start(s32[4,2]{0,1:T(2,128)} %param.7) | copy-start | bytes 100
  25.2 4.7 %collective-permute-start.4 = (f32[36,128]{1,0:T(8,128)S(1)}, f32[36,128]{1,0:T(8,128)S(1)}, u32[]{:S(2)}, u32[]{:S(2)}) collective-permute-start(f32[36,128]{1,0:T(8,128)S(1)} %get-tuple-element.21), channel_id=1, source_target_pairs={{0,8},{4,12},{8,0},{12,4},{1,9},{5,13},{9,1},{13,5},{2,10},{6,14},... | collective-permute-start | bytes 55304 | tf_op jit(solution)/shard_map/ppermute | solution.py:28
  26.1 5.6 %collective-permute-start.5 = (f32[36,128]{1,0:T(8,128)S(1)}, f32[36,128]{1,0:T(8,128)S(1)}, u32[]{:S(2)}, u32[]{:S(2)}) collective-permute-start(f32[36,128]{1,0:T(8,128)S(1)} %get-tuple-element.22), channel_id=1, source_target_pairs={{0,12},{4,8},{8,4},{12,0},{1,13},{5,9},{9,5},{13,1},{2,14},{6,10},... | collective-permute-start | bytes 55304 | tf_op jit(solution)/shard_map/ppermute | solution.py:28
  32.4 1.9 %collective-permute-start.6 = (f32[36,128]{1,0:T(8,128)S(1)}, f32[36,128]{1,0:T(8,128)S(1)}, u32[]{:S(2)}, u32[]{:S(2)}) collective-permute-start(f32[36,128]{1,0:T(8,128)S(1)} %get-tuple-element.24), channel_id=1, source_target_pairs={{0,1},{1,0},{2,3},{3,2},{4,5},{5,4},{6,7},{7,6},{8,9},{9,8},{10,11... | collective-permute-start | bytes 55304 | tf_op jit(solution)/shard_map/ppermute | solution.py:28
  32.4 3.8 %collective-permute-start.7 = (f32[36,128]{1,0:T(8,128)S(1)}, f32[36,128]{1,0:T(8,128)S(1)}, u32[]{:S(2)}, u32[]{:S(2)}) collective-permute-start(f32[36,128]{1,0:T(8,128)S(1)} %get-tuple-element.25), channel_id=1, source_target_pairs={{0,2},{1,3},{2,0},{3,1},{4,6},{5,7},{6,4},{7,5},{8,10},{9,11},{10,... | collective-permute-start | bytes 55304 | tf_op jit(solution)/shard_map/ppermute | solution.py:28
  34.0 3.2 %collective-permute-start.8 = (f32[36,128]{1,0:T(8,128)S(1)}, f32[36,128]{1,0:T(8,128)S(1)}, u32[]{:S(2)}, u32[]{:S(2)}) collective-permute-start(f32[36,128]{1,0:T(8,128)S(1)} %get-tuple-element.26), channel_id=1, source_target_pairs={{0,3},{1,2},{2,1},{3,0},{4,7},{5,6},{6,5},{7,4},{8,11},{9,10},{10,... | collective-permute-start | bytes 55304 | tf_op jit(solution)/shard_map/ppermute | solution.py:28

commit v2 on v1

--- a/solution.py
+++ b/solution.py
@@ -48,79 +48,114 @@
             out[pl.ds(d, 1), :] = tod_ref[d, pl.ds(segment, 1), :]
 
 
-def bin_kernel(count, lanes, upper, pad, rows, group, pix_ref, weight_ref, *refs):
+TILE = 16
+
+
+def spread(ref, c, d):
+    return ref[c, pl.ds(d, TILE, stride=0), :].astype(jnp.bfloat16)
+
+
+def numbers(count):
+    row = lax.broadcasted_iota(jnp.int32, (TILE, SPAN), 0).astype(jnp.float32)
+    return [(row + i).astype(jnp.bfloat16) for i in range(0, count, TILE)]
+
+
+def one_hot_sums(low_ref, high_ref, values, lows, highs, group):
+    spans, detectors, _ = low_ref.shape
+    low_number, high_number = numbers(lows), numbers(highs)
+    one = jnp.ones((TILE, SPAN), jnp.bfloat16)
+    zero = jnp.zeros((TILE, SPAN), jnp.bfloat16)
+
+    def step(g, totals):
+        sums = []
+        for c in range(spans):
+            left, right = [], []
+            for u in range(group):
+                d = g * group + u
+                low, high = spread(low_ref, c, d), spread(high_ref, c, d)
+                hot = [high == n for n in high_number]
+                left.append(
+                    jnp.concatenate([jnp.where(low == n, one, zero) for n in low_number], axis=0)
+                )
+                right.append(
+                    jnp.concatenate(
+                        [jnp.where(h, v(c, d, one), zero) for v in values for h in hot], axis=0
+                    )
+                )
+            binned = lax.dot_general(
+                jnp.concatenate(left, axis=1),
+                jnp.concatenate(right, axis=1),
+                (((1,), (1,)), ((), ())),
+                preferred_element_type=jnp.float32,
+            )
+            sums.append(binned if totals is None else totals[c] + binned)
+        return tuple(sums)
+
+    if detectors == group:
+        return step(0, None)
+    start = (jnp.zeros((lows, len(values) * highs), jnp.float32),) * spans
+    return lax.fori_loop(0, detectors // group, step, start)
+
+
+def divide(x, by):
+    quotient = ((x.astype(jnp.float32) + 0.5) * (1.0 / by)).astype(jnp.int32)
+    return quotient, x - quotient * by
+
+
+def ahead_kernel(lanes, upper, group, pix_ref, weight_ref, sums_ref, half_ref, row_ref, *scratch):
+    low_ref, high_ref, scale_ref = scratch
+    spans = low_ref.shape[0]
+    pad = -(-upper // TILE) * TILE
+    scale_ref[0] = weight_ref[...]
+    for c in range(spans):
+        high, low = divide(pix_ref[:, c * SPAN : (c + 1) * SPAN], lanes)
+        side, half = divide(low, lanes // 2)
+        low_ref[c] = low.astype(jnp.float32)
+        high_ref[c] = high.astype(jnp.float32)
+        half_ref[c] = half.astype(jnp.float32)
+        row_ref[c] = (side * upper + high).astype(jnp.float32)
+    values = [lambda c, d, one: spread(scale_ref, 0, d), lambda c, d, one: one]
+    totals = one_hot_sums(low_ref, high_ref, values, lanes, pad, group)
+    for c in range(spans):
+        turned = totals[c].T
+        for q in range(2):
+            sums_ref[c, q] = turned[q * pad : q * pad + upper]
+
+
+def value_kernel(count, lanes, upper, rows, group, weight_ref, sums_ref, half_ref, row_ref, *refs):
     parts, outs = refs[:count], refs[count : 2 * count]
-    value_ref, low_ref, high_ref, scale_ref, total_ref = refs[2 * count :]
+    value_ref, total_ref = refs[2 * count :]
     me = lax.axis_index("det")
     held, samples = parts[0].shape
     spans = samples // SPAN
     weight_all = jnp.sum(weight_ref[...], axis=0, keepdims=True)
     common = [jnp.zeros((1, SPAN), jnp.float32) for _ in range(spans)]
-    for step in range(count):
-        first = pl.multiple_of(source(me, step, count) * held, held)
-        weight = weight_ref[pl.ds(first, held), :]
-        scale_ref[0, step * held : (step + 1) * held, :] = weight
-        for c in range(spans):
-            common[c] += jnp.sum(
-                weight * parts[step][:, c * SPAN : (c + 1) * SPAN], axis=0, keepdims=True
-            )
-        for c in range(spans):
-            pix = pix_ref[pl.ds(first, held), c * SPAN : (c + 1) * SPAN]
-            high = ((pix.astype(jnp.float32) + 0.5) * (1.0 / lanes)).astype(jnp.int32)
-            low = pix - high * lanes
-            high_ref[c, step * held : (step + 1) * held, :] = high.astype(jnp.float32)
-            low_ref[c, step * held : (step + 1) * held, :] = low.astype(jnp.float32)
-    for step in range(count):
-        weight = scale_ref[0, step * held : (step + 1) * held, :]
-        for c in range(spans):
-            value_ref[c, step * held : (step + 1) * held, :] = weight * (
-                parts[step][:, c * SPAN : (c + 1) * SPAN] - common[c] / weight_all
-            )
-
-    tile = 16
-
-    def spread(ref, d, c):
-        return ref[c, pl.ds(d, tile, stride=0), :].astype(jnp.bfloat16)
-
-    number = lax.broadcasted_iota(jnp.int32, (tile, SPAN), 0).astype(jnp.float32)
-    low_number = [(number + i).astype(jnp.bfloat16) for i in range(0, lanes, tile)]
-    one = jnp.ones((tile, SPAN), jnp.bfloat16)
-    zero = jnp.zeros((tile, SPAN), jnp.bfloat16)
+    first = [pl.multiple_of(source(me, k, count) * held, held) for k in range(count)]
+    for k in range(count):
+        weight = weight_ref[pl.ds(first[k], held), :]
+        for c in range(spans):
+            part = parts[k][:, c * SPAN : (c + 1) * SPAN]
+            common[c] += jnp.sum(weight * part, axis=0, keepdims=True)
+    for k in range(count):
+        weight = weight_ref[pl.ds(first[k], held), :]
+        for c in range(spans):
+            part = parts[k][:, c * SPAN : (c + 1) * SPAN]
+            value_ref[c, pl.ds(first[k], held), :] = weight * (part - common[c] / weight_all)
+    values = [lambda c, d, one: spread(value_ref, c, d)]
+    highs = -(-2 * upper // TILE) * TILE
+    totals = one_hot_sums(half_ref, row_ref, values, lanes // 2, highs, group)
     for c in range(spans):
-
-        def step(g, acc):
-            left, right = [], []
-            for u in range(group):
-                d = g * group + u
-                low = spread(low_ref, d, c)
-                high = spread(high_ref, d, c)
-                value = spread(value_ref, d, c)
-                scale = spread(scale_ref, d, 0)
-                right.append(
-                    jnp.concatenate([jnp.where(low == n, one, zero) for n in low_number], axis=0)
-                )
-                hot = [high == n for n in low_number[: pad // tile]]
-                left.append(
-                    jnp.concatenate(
-                        [jnp.where(h, x, zero) for x in (value, scale, one) for h in hot], axis=0
-                    )
-                )
-            return acc + lax.dot_general(
-                jnp.concatenate(left, axis=1),
-                jnp.concatenate(right, axis=1),
-                (((1,), (1,)), ((), ())),
-                preferred_element_type=jnp.float32,
-            )
-
-        total_ref[c] = lax.fori_loop(
-            0, count * held // group, step, jnp.zeros((3 * pad, lanes), jnp.float32)
-        )
-    for step in range(count):
-        first = partner(me, step, count) * rows
-        for c in range(spans):
-            for q in range(3):
-                at = (c * 3 + q) * rows
-                outs[step][at : at + rows, :] = total_ref[c, pl.ds(q * pad + first, rows), :]
+        turned = totals[c].T
+        total_ref[c, :, : lanes // 2] = turned[:upper]
+        total_ref[c, :, lanes // 2 :] = turned[upper : 2 * upper]
+    for k in range(count):
+        to = partner(me, k, count) * rows
+        for c in range(spans):
+            at = c * 3 * rows
+            outs[k][at : at + rows, :] = total_ref[c, pl.ds(to, rows), :]
+            for q in range(2):
+                at = (c * 3 + q + 1) * rows
+                outs[k][at : at + rows, :] = sums_ref[c, q, pl.ds(to, rows), :]
 
 
 def place_kernel(count, blks, subs, spans, own, label_ref, *refs):
@@ -157,7 +192,6 @@
     lanes = max(n for n in range(1, 129) if width % n == 0)
     own = width // lanes
     upper = BLOCK_PIX // lanes
-    pad = -(-upper // 16) * 16
     f32 = jnp.float32
 
     cut = call(
@@ -173,19 +207,22 @@
     weight = jnp.broadcast_to(weight[:, None], (detectors, SPAN))
 
     rows = subs * own
+    group = min(detectors, 128)
+    index = jax.ShapeDtypeStruct((spans, detectors, SPAN), f32)
+    held_index = pltpu.VMEM((spans, detectors, SPAN), f32)
+    sums, half, row = call(
+        functools.partial(ahead_kernel, lanes, upper, min(group, 32)),
+        [jax.ShapeDtypeStruct((spans, 2, upper, lanes), f32), index, index],
+        [VMEM] * 2,
+        [held_index, held_index, pltpu.VMEM((1, detectors, SPAN), f32)],
+    )(pixels.reshape(detectors, samples), weight)
     shape = jax.ShapeDtypeStruct((spans * 3 * rows, lanes), f32)
     chunks = call(
-        functools.partial(bin_kernel, dets, lanes, upper, pad, rows, 4),
+        functools.partial(value_kernel, dets, lanes, upper, rows, group),
         [shape] * dets,
-        [VMEM] * (2 + dets),
-        [
-            pltpu.VMEM((spans, detectors, SPAN), f32),
-            pltpu.VMEM((spans, detectors, SPAN), f32),
-            pltpu.VMEM((spans, detectors, SPAN), f32),
-            pltpu.VMEM((1, detectors, SPAN), f32),
-            pltpu.VMEM((spans, 3 * pad, lanes), f32),
-        ],
-    )(pixels.reshape(detectors, samples), weight, *parts)
+        [VMEM] * (4 + dets),
+        [held_index, pltpu.VMEM((spans, upper, lanes), f32)],
+    )(weight, sums, half, row, *parts)
     chunks = [chunks[0]] + [exchange(chunks[k], "det", k, dets) for k in range(1, dets)]
 
     peers = blks * subs

time: 38 us -> 28.3 us (0.74)
  Pallas kernels: 12.7 us -> 5.15 us
  waiting for transfers between devices: 10.4 us -> 8.33 us
    pallas_call x1 -> x2, Pallas kernels: 12 us -> 4.38 us  [the longest x1 2.97 us: on_device(): call(functools.partial(ahead_kernel, lanes, upper, min(group, 32)), [jax....]
    ppermute x9, waiting for transfers between devices: 10.4 us -> 8.33 us  [exchange(): return lax.ppermute(x, axes, pairs)]
  transfers between devices with their start and end apart: 9 -> 9, of which waited for: 6 -> 5; matrix products, arithmetic and copies ran while one was open for 1% -> 1% of each run, Pallas kernels for 0% -> 11%
where the time goes in v2:
time: 28.3 us; the launch traced here: 28.1 us
  starting transfers between devices  12 us (42%)
  waiting for transfers between devices  8.33 us (29%)
  Pallas kernels  5.15 us (18%)
  local copies, waits for them, and re-layouts  1.79 us (6%)
  between operations  0.73 us (3%)
    ppermute x9, starting transfers between devices, exchange(): return lax.ppermute(x, axes, pairs)  12 us
    ppermute x9, waiting for transfers between devices, exchange(): return lax.ppermute(x, axes, pairs)  8.33 us
    pallas_call x1, Pallas kernels, on_device(): call(functools.partial(ahead_kernel, lanes, upper, min(group, 32)), [jax....  2.97 us
    pallas_call x1, Pallas kernels, on_device(): call(functools.partial(value_kernel, dets, lanes, upper, rows, group), [s...  1.41 us
    unnamed x12, local copies, waits for them, and re-layouts  1.02 us
    pallas_call x1, Pallas kernels, on_device(): call(functools.partial(place_kernel, dets, blks, subs, spans, own), [shap...  0.7 us
    squeeze x1, local copies, waits for them, and re-layouts, on_device(): return (total[0], total[1], total[2])  0.6 us
  transfers between devices with their start and end apart: 9, of which 5 were waited for; matrix products, arithmetic and copies ran while one was open for 1% of the time, Pallas kernels for 11%

profile of v2, /device:TPU:0, one launch (start us, length us, event | category | flops | bytes accessed | tf_op | source)
XLA Modules:
  0.0 28.1 jit_solution(422240203380048804)
XLA Ops:
  0.6 0.0 copy-start
  0.6 0.9 %copy-done = f32[32,4,256]{2,1,0:T(4,128)S(1)} copy-done((f32[32,4,256]{2,1,0:T(4,128)S(1)}, f32[32,4,256]{2,1,0:T(4,128)}, u32[]{:S(2)}) %copy-start) | copy-done | bytes 131096
  1.5 0.0 copy-start.1
  1.5 0.1 shard_map.77
  1.6 3.1 %collective-permute-start = (f32[32,256]{1,0:T(8,128)S(1)}, f32[32,256]{1,0:T(8,128)S(1)}, u32[]{:S(2)}, u32[]{:S(2)}) collective-permute-start(f32[32,256]{1,0:T(8,128)S(1)} %get-tuple-element.22), channel_id=1, source_target_pairs={{0,4},{4,0},{8,12},{12,8},{1,5},{5,1},{9,13},{13,9},{2,6},{6,2},{1... | collective-permute-start | bytes 98312 | tf_op jit(solution)/shard_map/ppermute | solution.py:28
  4.7 0.0 copy-start.3
  4.7 0.0 copy-start.4
  4.7 2.6 %collective-permute-start.1 = (f32[32,256]{1,0:T(8,128)S(1)}, f32[32,256]{1,0:T(8,128)S(1)}, u32[]{:S(2)}, u32[]{:S(2)}) collective-permute-start(f32[32,256]{1,0:T(8,128)S(1)} %get-tuple-element.23), channel_id=1, source_target_pairs={{0,8},{4,12},{8,0},{12,4},{1,9},{5,13},{9,1},{13,5},{2,10},{6,14},... | collective-permute-start | bytes 98312 | tf_op jit(solution)/shard_map/ppermute | solution.py:28
  7.3 0.0 collective-permute-start.2
  7.3 0.0 copy-done.3
  7.3 0.0 copy-done.4
  7.3 0.1 select_reduce_fusion
  7.4 0.0 copy-done.1
  7.4 0.1 broadcast_in_dim.2.weight_ref
  7.5 3.0 %shard_map.76 = (f32[2,2,24,128]{3,2,1,0:T(8,128)S(1)}, f32[2,128,128]{2,1,0:T(8,128)S(1)}, f32[2,128,128]{2,1,0:T(8,128)S(1)}) custom-call(s32[128,256]{1,0:T(8,128)S(1)} %bitcast.10, f32[128,128]{1,0:T(8,128)S(1)} %broadcast_in_dim.2.weight_ref), custom_call_target="tpu_custom_call" | custom-call | flops 1048576 | bytes 1048576 | tf_op jit(solution)/shard_map/pallas_call | solution.py:213
  10.5 0.0 collective-permute-done.refs_1_
  10.5 0.0 collective-permute-done.1.refs_2_
  10.5 2.5 %collective-permute-done.2.refs_3_ = f32[32,256]{1,0:T(8,128)S(1)} collective-permute-done((f32[32,256]{1,0:T(8,128)S(1)}, f32[32,256]{1,0:T(8,128)S(1)}, u32[]{:S(2)}, u32[]{:S(2)}) %collective-permute-start.2) | collective-permute-done | bytes 32800 | tf_op jit(solution)/shard_map/ppermute | solution.py:28
  13.0 1.4 %shard_map.78 = (f32[36,128]{1,0:T(8,128)S(1)}, f32[36,128]{1,0:T(8,128)S(1)}, f32[36,128]{1,0:T(8,128)S(1)}, f32[36,128]{1,0:T(8,128)S(1)}) custom-call(f32[128,128]{1,0:T(8,128)S(1)} %broadcast_in_dim.2.weight_ref, f32[2,2,24,128]{3,2,1,0:T(8,128)S(1)} %get-tuple-element.18.sums_ref, f32[2,128,128]{2,1,0:T(8,128)S(1)} %get-tuple-element.19.half_ref, ...), custom_call_target="tpu_custom_call" | custom-call | flops 1048576 | bytes 1048576 | tf_op jit(solution)/shard_map/pallas_call | solution.py:220
  14.4 0.0 collective-permute-start.3
  14.5 0.0 copy-start.2
  14.5 1.9 %collective-permute-start.4 = (f32[36,128]{1,0:T(8,128)S(1)}, f32[36,128]{1,0:T(8,128)S(1)}, u32[]{:S(2)}, u32[]{:S(2)}) collective-permute-start(f32[36,128]{1,0:T(8,128)S(1)} %get-tuple-element.27), channel_id=1, source_target_pairs={{0,8},{4,12},{8,0},{12,4},{1,9},{5,13},{9,1},{13,5},{2,10},{6,14},... | collective-permute-start | bytes 55304 | tf_op jit(solution)/shard_map/ppermute | solution.py:28
  16.3 2.5 %collective-permute-start.5 = (f32[36,128]{1,0:T(8,128)S(1)}, f32[36,128]{1,0:T(8,128)S(1)}, u32[]{:S(2)}, u32[]{:S(2)}) collective-permute-start(f32[36,128]{1,0:T(8,128)S(1)} %get-tuple-element.28), channel_id=1, source_target_pairs={{0,12},{4,8},{8,4},{12,0},{1,13},{5,9},{9,5},{13,1},{2,14},{6,10},... | collective-permute-start | bytes 55304 | tf_op jit(solution)/shard_map/ppermute | solution.py:28
  18.9 0.0 copy-done.2
  18.9 0.1 copy.13
  19.0 0.1 reshape.25.label_ref
  19.0 0.0 collective-permute-done.3.refs_1_
  19.0 0.2 collective-permute-done.4.refs_2_
  19.3 2.7 %collective-permute-done.5.refs_3_ = f32[36,128]{1,0:T(8,128)S(1)} collective-permute-done((f32[36,128]{1,0:T(8,128)S(1)}, f32[36,128]{1,0:T(8,128)S(1)}, u32[]{:S(2)}, u32[]{:S(2)}) %collective-permute-start.5) | collective-permute-done | bytes 18464 | tf_op jit(solution)/shard_map/ppermute | solution.py:28
  21.9 0.7 %shard_map.79 = (f32[36,128]{1,0:T(8,128)S(1)}, f32[36,128]{1,0:T(8,128)S(1)}, f32[36,128]{1,0:T(8,128)S(1)}, f32[36,128]{1,0:T(8,128)S(1)}) custom-call(s32[8]{0:T(128)S(1)} %reshape.25.label_ref, f32[36,128]{1,0:T(8,128)S(1)} %get-tuple-element.25.refs_0_, f32[36,128]{1,0:T(8,128)S(1)} %collective-permute-done.3.refs_1_, ...), custom_call_target="tpu_custom_call" | custom-call | flops 1048576 | bytes 1048576 | tf_op jit(solution)/shard_map/pallas_call | solution.py:230
  22.6 0.1 collective-permute-start.6
  22.7 1.5 %collective-permute-start.7 = (f32[36,128]{1,0:T(8,128)S(1)}, f32[36,128]{1,0:T(8,128)S(1)}, u32[]{:S(2)}, u32[]{:S(2)}) collective-permute-start(f32[36,128]{1,0:T(8,128)S(1)} %get-tuple-element.31), channel_id=1, source_target_pairs={{0,2},{1,3},{2,0},{3,1},{4,6},{5,7},{6,4},{7,5},{8,10},{9,11},{10,... | collective-permute-start | bytes 55304 | tf_op jit(solution)/shard_map/ppermute | solution.py:28
  24.3 0.3 %collective-permute-start.8 = (f32[36,128]{1,0:T(8,128)S(1)}, f32[36,128]{1,0:T(8,128)S(1)}, u32[]{:S(2)}, u32[]{:S(2)}) collective-permute-start(f32[36,128]{1,0:T(8,128)S(1)} %get-tuple-element.32), channel_id=1, source_target_pairs={{0,3},{1,2},{2,1},{3,0},{4,7},{5,6},{6,5},{7,4},{8,11},{9,10},{10,... | collective-permute-start | bytes 55304 | tf_op jit(solution)/shard_map/ppermute | solution.py:28
  24.6 0.0 collective-permute-done.6
  24.6 2.0 %collective-permute-done.7 = f32[36,128]{1,0:T(8,128)S(1)} collective-permute-done((f32[36,128]{1,0:T(8,128)S(1)}, f32[36,128]{1,0:T(8,128)S(1)}, u32[]{:S(2)}, u32[]{:S(2)}) %collective-permute-start.7) | collective-permute-done | bytes 18464 | tf_op jit(solution)/shard_map/ppermute | solution.py:28
  26.6 0.9 %collective-permute-done.8 = f32[36,128]{1,0:T(8,128)S(1)} collective-permute-done((f32[36,128]{1,0:T(8,128)S(1)}, f32[36,128]{1,0:T(8,128)S(1)}, u32[]{:S(2)}, u32[]{:S(2)}) %collective-permute-start.8) | collective-permute-done | bytes 18464 | tf_op jit(solution)/shard_map/ppermute | solution.py:28
  27.5 0.6 %slice_bitcast_fusion = (f32[4,384]{1,0:T(4,128)}, f32[4,384]{1,0:T(4,128)}, f32[4,384]{1,0:T(4,128)}) fusion(f32[3,4,3,128]{3,1,2,0:T(4,128)S(1)} %bitcast.11), kind=kLoop, calls=%fused_computation.2 | loop fusion | bytes 36864 | tf_op jit(solution)/shard_map/squeeze | solution.py:240
  (3 shorter events, 0.0 us)
Async XLA Ops:
  0.6 0.9 %copy-start = (f32[32,4,256]{2,1,0:T(4,128)S(1)}, f32[32,4,256]{2,1,0:T(4,128)}, u32[]{:S(2)}) copy-start(f32[32,4,256]{2,1,0:T(4,128)} %tod_ref.1) | copy-start | bytes 393220
  1.5 5.9 %copy-start.1 = (s32[128,1,256]{2,1,0:T(1,128)S(1)}, s32[128,1,256]{2,1,0:T(1,128)}, u32[]{:S(2)}) copy-start(s32[128,1,256]{2,1,0:T(1,128)} %param.6) | copy-start | bytes 393220
  1.6 8.9 %collective-permute-start = (f32[32,256]{1,0:T(8,128)S(1)}, f32[32,256]{1,0:T(8,128)S(1)}, u32[]{:S(2)}, u32[]{:S(2)}) collective-permute-start(f32[32,256]{1,0:T(8,128)S(1)} %get-tuple-element.22), channel_id=1, source_target_pairs={{0,4},{4,0},{8,12},{12,8},{1,5},{5,1},{9,13},{13,9},{2,6},{6,2},{1... | collective-permute-start | bytes 98312 | tf_op jit(solution)/shard_map/ppermute | solution.py:28
  4.7 2.6 %copy-start.3 = (f32[8]{0:T(128)S(1)}, f32[8]{0:T(128)}, u32[]{:S(2)}) copy-start(f32[8]{0:T(128)} %param.9) | copy-start | bytes 100
  4.7 2.6 %copy-start.4 = (s32[128]{0:T(128)S(1)}, s32[128]{0:T(128)}, u32[]{:S(2)}) copy-start(s32[128]{0:T(128)} %param.8) | copy-start | bytes 1540
  4.7 5.8 %collective-permute-start.1 = (f32[32,256]{1,0:T(8,128)S(1)}, f32[32,256]{1,0:T(8,128)S(1)}, u32[]{:S(2)}, u32[]{:S(2)}) collective-permute-start(f32[32,256]{1,0:T(8,128)S(1)} %get-tuple-element.23), channel_id=1, source_target_pairs={{0,8},{4,12},{8,0},{12,4},{1,9},{5,13},{9,1},{13,5},{2,10},{6,14},... | collective-permute-start | bytes 98312 | tf_op jit(solution)/shard_map/ppermute | solution.py:28
  7.3 5.7 %collective-permute-start.2 = (f32[32,256]{1,0:T(8,128)S(1)}, f32[32,256]{1,0:T(8,128)S(1)}, u32[]{:S(2)}, u32[]{:S(2)}) collective-permute-start(f32[32,256]{1,0:T(8,128)S(1)} %get-tuple-element.24), channel_id=1, source_target_pairs={{0,12},{4,8},{8,4},{12,0},{1,13},{5,9},{9,5},{13,1},{2,14},{6,10},... | collective-permute-start | bytes 98312 | tf_op jit(solution)/shard_map/ppermute | solution.py:28
  14.4 4.6 %collective-permute-start.3 = (f32[36,128]{1,0:T(8,128)S(1)}, f32[36,128]{1,0:T(8,128)S(1)}, u32[]{:S(2)}, u32[]{:S(2)}) collective-permute-start(f32[36,128]{1,0:T(8,128)S(1)} %get-tuple-element.26), channel_id=1, source_target_pairs={{0,4},{4,0},{8,12},{12,8},{1,5},{5,1},{9,13},{13,9},{2,6},{6,2},{1... | collective-permute-start | bytes 55304 | tf_op jit(solution)/shard_map/ppermute | solution.py:28
  14.5 4.4 %copy-start.2 = (s32[4,2]{0,1:T(2,128)S(1)}, s32[4,2]{0,1:T(2,128)}, u32[]{:S(2)}) copy-start(s32[4,2]{0,1:T(2,128)} %param.7) | copy-start | bytes 100
  14.5 4.8 %collective-permute-start.4 = (f32[36,128]{1,0:T(8,128)S(1)}, f32[36,128]{1,0:T(8,128)S(1)}, u32[]{:S(2)}, u32[]{:S(2)}) collective-permute-start(f32[36,128]{1,0:T(8,128)S(1)} %get-tuple-element.27), channel_id=1, source_target_pairs={{0,8},{4,12},{8,0},{12,4},{1,9},{5,13},{9,1},{13,5},{2,10},{6,14},... | collective-permute-start | bytes 55304 | tf_op jit(solution)/shard_map/ppermute | solution.py:28
  16.3 5.6 %collective-permute-start.5 = (f32[36,128]{1,0:T(8,128)S(1)}, f32[36,128]{1,0:T(8,128)S(1)}, u32[]{:S(2)}, u32[]{:S(2)}) collective-permute-start(f32[36,128]{1,0:T(8,128)S(1)} %get-tuple-element.28), channel_id=1, source_target_pairs={{0,12},{4,8},{8,4},{12,0},{1,13},{5,9},{9,5},{13,1},{2,14},{6,10},... | collective-permute-start | bytes 55304 | tf_op jit(solution)/shard_map/ppermute | solution.py:28
  22.6 1.9 %collective-permute-start.6 = (f32[36,128]{1,0:T(8,128)S(1)}, f32[36,128]{1,0:T(8,128)S(1)}, u32[]{:S(2)}, u32[]{:S(2)}) collective-permute-start(f32[36,128]{1,0:T(8,128)S(1)} %get-tuple-element.30), channel_id=1, source_target_pairs={{0,1},{1,0},{2,3},{3,2},{4,5},{5,4},{6,7},{7,6},{8,9},{9,8},{10,11... | collective-permute-start | bytes 55304 | tf_op jit(solution)/shard_map/ppermute | solution.py:28
  22.7 3.8 %collective-permute-start.7 = (f32[36,128]{1,0:T(8,128)S(1)}, f32[36,128]{1,0:T(8,128)S(1)}, u32[]{:S(2)}, u32[]{:S(2)}) collective-permute-start(f32[36,128]{1,0:T(8,128)S(1)} %get-tuple-element.31), channel_id=1, source_target_pairs={{0,2},{1,3},{2,0},{3,1},{4,6},{5,7},{6,4},{7,5},{8,10},{9,11},{10,... | collective-permute-start | bytes 55304 | tf_op jit(solution)/shard_map/ppermute | solution.py:28
  24.3 3.2 %collective-permute-start.8 = (f32[36,128]{1,0:T(8,128)S(1)}, f32[36,128]{1,0:T(8,128)S(1)}, u32[]{:S(2)}, u32[]{:S(2)}) collective-permute-start(f32[36,128]{1,0:T(8,128)S(1)} %get-tuple-element.32), channel_id=1, source_target_pairs={{0,3},{1,2},{2,1},{3,0},{4,7},{5,6},{6,5},{7,4},{8,11},{9,10},{10,... | collective-permute-start | bytes 55304 | tf_op jit(solution)/shard_map/ppermute | solution.py:28

commit v3 on v2

--- a/solution.py
+++ b/solution.py
@@ -7,23 +7,24 @@
 from jax.experimental.pallas import tpu as pltpu
 from jax.sharding import PartitionSpec as P
 
+
 BLOCK_PIX = 3072
 SPAN = 128
 BLK_OWN = 4
+XOR = {"tod": True, "bins": False, "maps": True}
 VMEM = pltpu.MemorySpace.VMEM
-SMEM = pltpu.MemorySpace.SMEM
-
-
-def partner(index, step, count):
-    return index ^ step if count & (count - 1) == 0 else lax.rem(index + step, count)
-
-
-def source(index, step, count):
-    return index ^ step if count & (count - 1) == 0 else lax.rem(index + count - step, count)
-
-
-def exchange(x, axes, step, count):
-    power = count & (count - 1) == 0
+
+
+def partner(name, index, step, count):
+    return index ^ step if XOR[name] else lax.rem(index + step, count)
+
+
+def source(name, index, step, count):
+    return index ^ step if XOR[name] else lax.rem(index + count - step, count)
+
+
+def exchange(name, x, axes, step, count):
+    power = XOR[name]
     pairs = [(i, i ^ step if power else (i + step) % count) for i in range(count)]
     return lax.ppermute(x, axes, pairs)
 
@@ -43,7 +44,7 @@
 def cut_kernel(count, tod_ref, *outs):
     me = lax.axis_index("det")
     for step, out in enumerate(outs):
-        segment = partner(me, step, count)
+        segment = partner("tod", me, step, count)
         for d in range(tod_ref.shape[0]):
             out[pl.ds(d, 1), :] = tod_ref[d, pl.ds(segment, 1), :]
 
@@ -105,21 +106,24 @@
 def ahead_kernel(lanes, upper, group, pix_ref, weight_ref, sums_ref, half_ref, row_ref, *scratch):
     low_ref, high_ref, scale_ref = scratch
     spans = low_ref.shape[0]
-    pad = -(-upper // TILE) * TILE
+    wide = lanes // 4
+    pad = -(-wide // TILE) * TILE
     scale_ref[0] = weight_ref[...]
     for c in range(spans):
-        high, low = divide(pix_ref[:, c * SPAN : (c + 1) * SPAN], lanes)
-        side, half = divide(low, lanes // 2)
-        low_ref[c] = low.astype(jnp.float32)
-        high_ref[c] = high.astype(jnp.float32)
+        row, lane = divide(pix_ref[:, c * SPAN : (c + 1) * SPAN], lanes)
+        side, half = divide(lane, 2 * wide)
+        quarter, rest = divide(lane, wide)
+        low_ref[c] = (quarter * upper + row).astype(jnp.float32)
+        high_ref[c] = rest.astype(jnp.float32)
         half_ref[c] = half.astype(jnp.float32)
-        row_ref[c] = (side * upper + high).astype(jnp.float32)
+        row_ref[c] = (side * upper + row).astype(jnp.float32)
     values = [lambda c, d, one: spread(scale_ref, 0, d), lambda c, d, one: one]
-    totals = one_hot_sums(low_ref, high_ref, values, lanes, pad, group)
+    totals = one_hot_sums(low_ref, high_ref, values, 4 * upper, pad, group)
     for c in range(spans):
-        turned = totals[c].T
         for q in range(2):
-            sums_ref[c, q] = turned[q * pad : q * pad + upper]
+            for i in range(4):
+                part = totals[c][i * upper : (i + 1) * upper, q * pad : q * pad + wide]
+                sums_ref[c, q, :, i * wide : (i + 1) * wide] = part
 
 
 def value_kernel(count, lanes, upper, rows, group, weight_ref, sums_ref, half_ref, row_ref, *refs):
@@ -130,7 +134,7 @@
     spans = samples // SPAN
     weight_all = jnp.sum(weight_ref[...], axis=0, keepdims=True)
     common = [jnp.zeros((1, SPAN), jnp.float32) for _ in range(spans)]
-    first = [pl.multiple_of(source(me, k, count) * held, held) for k in range(count)]
+    first = [pl.multiple_of(source("tod", me, k, count) * held, held) for k in range(count)]
     for k in range(count):
         weight = weight_ref[pl.ds(first[k], held), :]
         for c in range(spans):
@@ -149,7 +153,7 @@
         total_ref[c, :, : lanes // 2] = turned[:upper]
         total_ref[c, :, lanes // 2 :] = turned[upper : 2 * upper]
     for k in range(count):
-        to = partner(me, k, count) * rows
+        to = partner("bins", me, k, count) * rows
         for c in range(spans):
             at = c * 3 * rows
             outs[k][at : at + rows, :] = total_ref[c, pl.ds(to, rows), :]
@@ -159,28 +163,36 @@
 
 
 def place_kernel(count, blks, subs, spans, own, label_ref, *refs):
-    parts, outs = refs[:count], refs[count:]
+    parts, outs, total_ref = refs[:count], refs[count:-1], refs[-1]
     me = lax.axis_index("det")
-    lanes = parts[0].shape[1]
+    blocks, lanes = total_ref.shape[1:]
     here = lax.axis_index("blk") * subs + lax.axis_index("sub")
+    number = lax.broadcasted_iota(jnp.int32, (blocks, lanes), 0)
+    masks = [
+        [
+            number == label_ref[pl.ds(source("bins", me, k, count) * spans + c, blocks, stride=0), :]
+            for c in range(spans)
+        ]
+        for k in range(count)
+    ]
+    rows = 3 * subs * own
+    for row in range(rows):
+        terms = [
+            jnp.where(masks[k][c], parts[k][pl.ds(c * rows + row, blocks, stride=0), :], 0.0)
+            for k in range(count)
+            for c in range(spans)
+        ]
+        while len(terms) > 1:
+            terms = [sum(terms[i : i + 2]) for i in range(0, len(terms), 2)]
+        total_ref[row] = terms[0]
     for step, out in enumerate(outs):
-        to = partner(here, step, blks * subs)
-        block, sub = to // subs, lax.rem(to, subs)
-        number = lax.broadcasted_iota(jnp.int32, (BLK_OWN, lanes), 0) + block * BLK_OWN
-        masks = [
-            [number == label_ref[source(me, k, count) * spans + c] for c in range(spans)]
-            for k in range(count)
-        ]
+        to = partner("maps", here, step, blks * subs)
+        first, sub = to // subs * BLK_OWN, lax.rem(to, subs)
         for q in range(3):
             for r in range(own):
-                total = jnp.zeros((BLK_OWN, lanes), jnp.float32)
-                for k in range(count):
-                    for c in range(spans):
-                        row = (c * 3 + q) * subs * own + sub * own + r
-                        part = parts[k][pl.ds(row, BLK_OWN, stride=0), :]
-                        total += jnp.where(masks[k][c], part, 0.0)
                 at = (q * own + r) * BLK_OWN
-                out[at : at + BLK_OWN, :] = total
+                row = (q * subs + sub) * own + r
+                out[at : at + BLK_OWN, :] = total_ref[row, pl.ds(first, BLK_OWN), :]
 
 
 def on_device(tod, pixels, span_block, weight_class, class_weight):
@@ -199,7 +211,7 @@
         [jax.ShapeDtypeStruct((held, samples), f32)] * dets,
         [VMEM],
     )(tod)
-    parts = [cut[0]] + [exchange(cut[k], "det", k, dets) for k in range(1, dets)]
+    parts = [cut[0]] + [exchange("tod", cut[k], "det", k, dets) for k in range(1, dets)]
 
     classes = jnp.arange(class_weight.shape[0], dtype=jnp.int32)
     picker = (weight_class[:, None] == classes[None, :]).astype(f32)
@@ -211,7 +223,7 @@
     index = jax.ShapeDtypeStruct((spans, detectors, SPAN), f32)
     held_index = pltpu.VMEM((spans, detectors, SPAN), f32)
     sums, half, row = call(
-        functools.partial(ahead_kernel, lanes, upper, min(group, 32)),
+        functools.partial(ahead_kernel, lanes, upper, group),
         [jax.ShapeDtypeStruct((spans, 2, upper, lanes), f32), index, index],
         [VMEM] * 2,
         [held_index, held_index, pltpu.VMEM((1, detectors, SPAN), f32)],
@@ -223,18 +235,19 @@
         [VMEM] * (4 + dets),
         [held_index, pltpu.VMEM((spans, upper, lanes), f32)],
     )(weight, sums, half, row, *parts)
-    chunks = [chunks[0]] + [exchange(chunks[k], "det", k, dets) for k in range(1, dets)]
+    chunks = [chunks[0]] + [exchange("bins", chunks[k], "det", k, dets) for k in range(1, dets)]
 
     peers = blks * subs
     shape = jax.ShapeDtypeStruct((3 * own * BLK_OWN, lanes), f32)
     placed = call(
         functools.partial(place_kernel, dets, blks, subs, spans, own),
         [shape] * peers,
-        [SMEM] + [VMEM] * dets,
-    )(span_block.reshape(-1), *chunks)
+        [VMEM] * (1 + dets),
+        [pltpu.VMEM((3 * rows, BLK_OWN * blks, lanes), f32)],
+    )(jnp.broadcast_to(span_block.reshape(-1, 1), (span_block.size, lanes)), *chunks)
     total = placed[0]
     for k in range(1, peers):
-        total = total + exchange(placed[k], ("blk", "sub"), k, peers)
+        total = total + exchange("maps", placed[k], ("blk", "sub"), k, peers)
     total = total.reshape(3, own, BLK_OWN, lanes).transpose(0, 2, 1, 3)
     total = total.reshape(3, BLK_OWN, width)
     return total[0], total[1], total[2]

time: 28.3 us -> 26.4 us (0.933)
  Pallas kernels: 5.15 us -> 3.43 us
  starting transfers between devices: 12 us -> 11.4 us
  waiting for transfers between devices: 8.33 us -> 8.68 us
    pallas_call x1, Pallas kernels: 2.97 us -> 1.88 us  [on_device(): call(functools.partial(ahead_kernel, lanes, upper, group), [jax.ShapeDtyp...]
    pallas_call x1, Pallas kernels: 0.7 us -> 0.06 us  [on_device(): call(functools.partial(place_kernel, dets, blks, subs, spans, own), [shap...]
    ppermute x9, starting transfers between devices: 12 us -> 11.4 us  [exchange(): return lax.ppermute(x, axes, pairs)]
    ppermute x9, waiting for transfers between devices: 8.33 us -> 8.68 us  [exchange(): return lax.ppermute(x, axes, pairs)]
  transfers between devices with their start and end apart: 9 -> 9, of which waited for: 5 -> 6; matrix products, arithmetic and copies ran while one was open for 1% -> 1% of each run, Pallas kernels for 11% -> 7%
where the time goes in v3:
time: 26.4 us; the launch traced here: 26.2 us
  starting transfers between devices  11.4 us (43%)
  waiting for transfers between devices  8.68 us (33%)
  Pallas kernels  3.43 us (13%)
  local copies, waits for them, and re-layouts  1.86 us (7%)
  between operations  0.72 us (3%)
    ppermute x9, starting transfers between devices, exchange(): return lax.ppermute(x, axes, pairs)  11.4 us
    ppermute x9, waiting for transfers between devices, exchange(): return lax.ppermute(x, axes, pairs)  8.68 us
    pallas_call x1, Pallas kernels, on_device(): call(functools.partial(ahead_kernel, lanes, upper, group), [jax.ShapeDtyp...  1.88 us
    pallas_call x1, Pallas kernels, on_device(): call(functools.partial(value_kernel, dets, lanes, upper, rows, group), [s...  1.41 us
    unnamed x12, local copies, waits for them, and re-layouts  1.02 us
    squeeze x1, local copies, waits for them, and re-layouts, on_device(): return (total[0], total[1], total[2])  0.6 us
  transfers between devices with their start and end apart: 9, of which 6 were waited for; matrix products, arithmetic and copies ran while one was open for 1% of the time, Pallas kernels for 7%

profile of v3, /device:TPU:0, one launch (start us, length us, event | category | flops | bytes accessed | tf_op | source)
XLA Modules:
  0.0 26.2 jit_solution(17348010215649812313)
XLA Ops:
  0.6 0.0 copy-start
  0.6 0.9 %copy-done = f32[32,4,256]{2,1,0:T(4,128)S(1)} copy-done((f32[32,4,256]{2,1,0:T(4,128)S(1)}, f32[32,4,256]{2,1,0:T(4,128)}, u32[]{:S(2)}) %copy-start) | copy-done | bytes 131096
  1.5 0.0 copy-start.1
  1.5 0.1 shard_map.77
  1.6 3.1 %collective-permute-start = (f32[32,256]{1,0:T(8,128)S(1)}, f32[32,256]{1,0:T(8,128)S(1)}, u32[]{:S(2)}, u32[]{:S(2)}) collective-permute-start(f32[32,256]{1,0:T(8,128)S(1)} %get-tuple-element.22), channel_id=1, source_target_pairs={{0,4},{4,0},{8,12},{12,8},{1,5},{5,1},{9,13},{13,9},{2,6},{6,2},{1... | collective-permute-start | bytes 98312 | tf_op jit(solution)/shard_map/ppermute | solution.py:29
  4.7 0.0 copy-start.3
  4.7 0.0 copy-start.4
  4.7 2.6 %collective-permute-start.1 = (f32[32,256]{1,0:T(8,128)S(1)}, f32[32,256]{1,0:T(8,128)S(1)}, u32[]{:S(2)}, u32[]{:S(2)}) collective-permute-start(f32[32,256]{1,0:T(8,128)S(1)} %get-tuple-element.23), channel_id=1, source_target_pairs={{0,8},{4,12},{8,0},{12,4},{1,9},{5,13},{9,1},{13,5},{2,10},{6,14},... | collective-permute-start | bytes 98312 | tf_op jit(solution)/shard_map/ppermute | solution.py:29
  7.3 0.0 collective-permute-start.2
  7.3 0.0 copy-done.3
  7.3 0.0 copy-done.4
  7.3 0.1 select_reduce_fusion
  7.4 0.0 copy-done.1
  7.4 0.1 broadcast_in_dim.8.weight_ref
  7.5 1.9 %shard_map.76 = (f32[2,2,24,128]{3,2,1,0:T(8,128)S(1)}, f32[2,128,128]{2,1,0:T(8,128)S(1)}, f32[2,128,128]{2,1,0:T(8,128)S(1)}) custom-call(s32[128,256]{1,0:T(8,128)S(1)} %bitcast.10, f32[128,128]{1,0:T(8,128)S(1)} %broadcast_in_dim.8.weight_ref), custom_call_target="tpu_custom_call" | custom-call | flops 1048576 | bytes 1048576 | tf_op jit(solution)/shard_map/pallas_call | solution.py:225
  9.4 0.0 collective-permute-done.refs_1_
  9.4 0.7 %collective-permute-done.1.refs_2_ = f32[32,256]{1,0:T(8,128)S(1)} collective-permute-done((f32[32,256]{1,0:T(8,128)S(1)}, f32[32,256]{1,0:T(8,128)S(1)}, u32[]{:S(2)}, u32[]{:S(2)}) %collective-permute-start.1) | collective-permute-done | bytes 32800 | tf_op jit(solution)/shard_map/ppermute | solution.py:29
  10.1 2.9 %collective-permute-done.2.refs_3_ = f32[32,256]{1,0:T(8,128)S(1)} collective-permute-done((f32[32,256]{1,0:T(8,128)S(1)}, f32[32,256]{1,0:T(8,128)S(1)}, u32[]{:S(2)}, u32[]{:S(2)}) %collective-permute-start.2) | collective-permute-done | bytes 32800 | tf_op jit(solution)/shard_map/ppermute | solution.py:29
  13.0 1.4 %shard_map.78 = (f32[36,128]{1,0:T(8,128)S(1)}, f32[36,128]{1,0:T(8,128)S(1)}, f32[36,128]{1,0:T(8,128)S(1)}, f32[36,128]{1,0:T(8,128)S(1)}) custom-call(f32[128,128]{1,0:T(8,128)S(1)} %broadcast_in_dim.8.weight_ref, f32[2,2,24,128]{3,2,1,0:T(8,128)S(1)} %get-tuple-element.18.sums_ref, f32[2,128,128]{2,1,0:T(8,128)S(1)} %get-tuple-element.19.half_ref, ...), custom_call_target="tpu_custom_call" | custom-call | flops 1048576 | bytes 1048576 | tf_op jit(solution)/shard_map/pallas_call | solution.py:232
  14.4 0.0 collective-permute-start.3
  14.5 0.0 copy-start.2
  14.5 0.9 %collective-permute-start.4 = (f32[36,128]{1,0:T(8,128)S(1)}, f32[36,128]{1,0:T(8,128)S(1)}, u32[]{:S(2)}, u32[]{:S(2)}) collective-permute-start(f32[36,128]{1,0:T(8,128)S(1)} %get-tuple-element.27), channel_id=1, source_target_pairs={{0,8},{4,12},{8,0},{12,4},{1,9},{5,13},{9,1},{13,5},{2,10},{6,14},... | collective-permute-start | bytes 55304 | tf_op jit(solution)/shard_map/ppermute | solution.py:29
  15.4 2.9 %collective-permute-start.5 = (f32[36,128]{1,0:T(8,128)S(1)}, f32[36,128]{1,0:T(8,128)S(1)}, u32[]{:S(2)}, u32[]{:S(2)}) collective-permute-start(f32[36,128]{1,0:T(8,128)S(1)} %get-tuple-element.28), channel_id=1, source_target_pairs={{0,12},{4,0},{8,4},{12,8},{1,13},{5,1},{9,5},{13,9},{2,14},{6,2},{... | collective-permute-start | bytes 55304 | tf_op jit(solution)/shard_map/ppermute | solution.py:29
  18.3 0.0 copy-done.2
  18.3 0.1 copy.13
  18.4 0.1 broadcast_in_dim.6
  18.5 1.6 %collective-permute-done.3.refs_1_ = f32[36,128]{1,0:T(8,128)S(1)} collective-permute-done((f32[36,128]{1,0:T(8,128)S(1)}, f32[36,128]{1,0:T(8,128)S(1)}, u32[]{:S(2)}, u32[]{:S(2)}) %collective-permute-start.3) | collective-permute-done | bytes 18464 | tf_op jit(solution)/shard_map/ppermute | solution.py:29
  20.0 0.0 collective-permute-done.4.refs_2_
  20.0 0.6 %collective-permute-done.5.refs_3_ = f32[36,128]{1,0:T(8,128)S(1)} collective-permute-done((f32[36,128]{1,0:T(8,128)S(1)}, f32[36,128]{1,0:T(8,128)S(1)}, u32[]{:S(2)}, u32[]{:S(2)}) %collective-permute-start.5) | collective-permute-done | bytes 18464 | tf_op jit(solution)/shard_map/ppermute | solution.py:29
  20.6 0.1 broadcast_in_dim.7.label_ref
  20.7 0.1 shard_map.79
  20.8 0.1 collective-permute-start.6
  20.8 1.6 %collective-permute-start.7 = (f32[36,128]{1,0:T(8,128)S(1)}, f32[36,128]{1,0:T(8,128)S(1)}, u32[]{:S(2)}, u32[]{:S(2)}) collective-permute-start(f32[36,128]{1,0:T(8,128)S(1)} %get-tuple-element.31), channel_id=1, source_target_pairs={{0,2},{1,3},{2,0},{3,1},{4,6},{5,7},{6,4},{7,5},{8,10},{9,11},{10,... | collective-permute-start | bytes 55304 | tf_op jit(solution)/shard_map/ppermute | solution.py:29
  22.4 0.3 %collective-permute-start.8 = (f32[36,128]{1,0:T(8,128)S(1)}, f32[36,128]{1,0:T(8,128)S(1)}, u32[]{:S(2)}, u32[]{:S(2)}) collective-permute-start(f32[36,128]{1,0:T(8,128)S(1)} %get-tuple-element.32), channel_id=1, source_target_pairs={{0,3},{1,2},{2,1},{3,0},{4,7},{5,6},{6,5},{7,4},{8,11},{9,10},{10,... | collective-permute-start | bytes 55304 | tf_op jit(solution)/shard_map/ppermute | solution.py:29
  22.7 0.0 collective-permute-done.6
  22.7 2.0 %collective-permute-done.7 = f32[36,128]{1,0:T(8,128)S(1)} collective-permute-done((f32[36,128]{1,0:T(8,128)S(1)}, f32[36,128]{1,0:T(8,128)S(1)}, u32[]{:S(2)}, u32[]{:S(2)}) %collective-permute-start.7) | collective-permute-done | bytes 18464 | tf_op jit(solution)/shard_map/ppermute | solution.py:29
  24.7 0.9 %collective-permute-done.8 = f32[36,128]{1,0:T(8,128)S(1)} collective-permute-done((f32[36,128]{1,0:T(8,128)S(1)}, f32[36,128]{1,0:T(8,128)S(1)}, u32[]{:S(2)}, u32[]{:S(2)}) %collective-permute-start.8) | collective-permute-done | bytes 18464 | tf_op jit(solution)/shard_map/ppermute | solution.py:29
  25.6 0.6 %slice_bitcast_fusion = (f32[4,384]{1,0:T(4,128)}, f32[4,384]{1,0:T(4,128)}, f32[4,384]{1,0:T(4,128)}) fusion(f32[3,4,3,128]{3,1,2,0:T(4,128)S(1)} %bitcast.11), kind=kLoop, calls=%fused_computation.2 | loop fusion | bytes 36864 | tf_op jit(solution)/shard_map/squeeze | solution.py:253
  (3 shorter events, 0.0 us)
Async XLA Ops:
  0.6 0.9 %copy-start = (f32[32,4,256]{2,1,0:T(4,128)S(1)}, f32[32,4,256]{2,1,0:T(4,128)}, u32[]{:S(2)}) copy-start(f32[32,4,256]{2,1,0:T(4,128)} %tod_ref.1) | copy-start | bytes 393220
  1.5 5.9 %copy-start.1 = (s32[128,1,256]{2,1,0:T(1,128)S(1)}, s32[128,1,256]{2,1,0:T(1,128)}, u32[]{:S(2)}) copy-start(s32[128,1,256]{2,1,0:T(1,128)} %param.6) | copy-start | bytes 393220
  1.6 7.8 %collective-permute-start = (f32[32,256]{1,0:T(8,128)S(1)}, f32[32,256]{1,0:T(8,128)S(1)}, u32[]{:S(2)}, u32[]{:S(2)}) collective-permute-start(f32[32,256]{1,0:T(8,128)S(1)} %get-tuple-element.22), channel_id=1, source_target_pairs={{0,4},{4,0},{8,12},{12,8},{1,5},{5,1},{9,13},{13,9},{2,6},{6,2},{1... | collective-permute-start | bytes 98312 | tf_op jit(solution)/shard_map/ppermute | solution.py:29
  4.7 2.6 %copy-start.3 = (f32[8]{0:T(128)S(1)}, f32[8]{0:T(128)}, u32[]{:S(2)}) copy-start(f32[8]{0:T(128)} %param.9) | copy-start | bytes 100
  4.7 2.6 %copy-start.4 = (s32[128]{0:T(128)S(1)}, s32[128]{0:T(128)}, u32[]{:S(2)}) copy-start(s32[128]{0:T(128)} %param.8) | copy-start | bytes 1540
  4.7 5.4 %collective-permute-start.1 = (f32[32,256]{1,0:T(8,128)S(1)}, f32[32,256]{1,0:T(8,128)S(1)}, u32[]{:S(2)}, u32[]{:S(2)}) collective-permute-start(f32[32,256]{1,0:T(8,128)S(1)} %get-tuple-element.23), channel_id=1, source_target_pairs={{0,8},{4,12},{8,0},{12,4},{1,9},{5,13},{9,1},{13,5},{2,10},{6,14},... | collective-permute-start | bytes 98312 | tf_op jit(solution)/shard_map/ppermute | solution.py:29
  7.3 5.7 %collective-permute-start.2 = (f32[32,256]{1,0:T(8,128)S(1)}, f32[32,256]{1,0:T(8,128)S(1)}, u32[]{:S(2)}, u32[]{:S(2)}) collective-permute-start(f32[32,256]{1,0:T(8,128)S(1)} %get-tuple-element.24), channel_id=1, source_target_pairs={{0,12},{4,8},{8,4},{12,0},{1,13},{5,9},{9,5},{13,1},{2,14},{6,10},... | collective-permute-start | bytes 98312 | tf_op jit(solution)/shard_map/ppermute | solution.py:29
  14.4 5.6 %collective-permute-start.3 = (f32[36,128]{1,0:T(8,128)S(1)}, f32[36,128]{1,0:T(8,128)S(1)}, u32[]{:S(2)}, u32[]{:S(2)}) collective-permute-start(f32[36,128]{1,0:T(8,128)S(1)} %get-tuple-element.26), channel_id=1, source_target_pairs={{0,4},{4,8},{8,12},{12,0},{1,5},{5,9},{9,13},{13,1},{2,6},{6,10},{... | collective-permute-start | bytes 55304 | tf_op jit(solution)/shard_map/ppermute | solution.py:29
  14.5 3.8 %copy-start.2 = (s32[4,2]{0,1:T(2,128)S(1)}, s32[4,2]{0,1:T(2,128)}, u32[]{:S(2)}) copy-start(s32[4,2]{0,1:T(2,128)} %param.7) | copy-start | bytes 100
  14.5 5.6 %collective-permute-start.4 = (f32[36,128]{1,0:T(8,128)S(1)}, f32[36,128]{1,0:T(8,128)S(1)}, u32[]{:S(2)}, u32[]{:S(2)}) collective-permute-start(f32[36,128]{1,0:T(8,128)S(1)} %get-tuple-element.27), channel_id=1, source_target_pairs={{0,8},{4,12},{8,0},{12,4},{1,9},{5,13},{9,1},{13,5},{2,10},{6,14},... | collective-permute-start | bytes 55304 | tf_op jit(solution)/shard_map/ppermute | solution.py:29
  15.4 5.2 %collective-permute-start.5 = (f32[36,128]{1,0:T(8,128)S(1)}, f32[36,128]{1,0:T(8,128)S(1)}, u32[]{:S(2)}, u32[]{:S(2)}) collective-permute-start(f32[36,128]{1,0:T(8,128)S(1)} %get-tuple-element.28), channel_id=1, source_target_pairs={{0,12},{4,0},{8,4},{12,8},{1,13},{5,1},{9,5},{13,9},{2,14},{6,2},{... | collective-permute-start | bytes 55304 | tf_op jit(solution)/shard_map/ppermute | solution.py:29
  20.8 1.9 %collective-permute-start.6 = (f32[36,128]{1,0:T(8,128)S(1)}, f32[36,128]{1,0:T(8,128)S(1)}, u32[]{:S(2)}, u32[]{:S(2)}) collective-permute-start(f32[36,128]{1,0:T(8,128)S(1)} %get-tuple-element.30), channel_id=1, source_target_pairs={{0,1},{1,0},{2,3},{3,2},{4,5},{5,4},{6,7},{7,6},{8,9},{9,8},{10,11... | collective-permute-start | bytes 55304 | tf_op jit(solution)/shard_map/ppermute | solution.py:29
  20.8 3.8 %collective-permute-start.7 = (f32[36,128]{1,0:T(8,128)S(1)}, f32[36,128]{1,0:T(8,128)S(1)}, u32[]{:S(2)}, u32[]{:S(2)}) collective-permute-start(f32[36,128]{1,0:T(8,128)S(1)} %get-tuple-element.31), channel_id=1, source_target_pairs={{0,2},{1,3},{2,0},{3,1},{4,6},{5,7},{6,4},{7,5},{8,10},{9,11},{10,... | collective-permute-start | bytes 55304 | tf_op jit(solution)/shard_map/ppermute | solution.py:29
  22.4 3.2 %collective-permute-start.8 = (f32[36,128]{1,0:T(8,128)S(1)}, f32[36,128]{1,0:T(8,128)S(1)}, u32[]{:S(2)}, u32[]{:S(2)}) collective-permute-start(f32[36,128]{1,0:T(8,128)S(1)} %get-tuple-element.32), channel_id=1, source_target_pairs={{0,3},{1,2},{2,1},{3,0},{4,7},{5,6},{6,5},{7,4},{8,11},{9,10},{10,... | collective-permute-start | bytes 55304 | tf_op jit(solution)/shard_map/ppermute | solution.py:29

commit v4 on v3

--- a/solution.py
+++ b/solution.py
@@ -11,21 +11,27 @@
 BLOCK_PIX = 3072
 SPAN = 128
 BLK_OWN = 4
-XOR = {"tod": True, "bins": False, "maps": True}
+XOR = {"tod": True, "bins": False, "maps": True, "label": True}
 VMEM = pltpu.MemorySpace.VMEM
 
 
+def paired(name, count):
+    return XOR.get(name, True) and count & (count - 1) == 0
+
+
 def partner(name, index, step, count):
-    return index ^ step if XOR[name] else lax.rem(index + step, count)
+    return index ^ step if paired(name, count) else lax.rem(index + step, count)
 
 
 def source(name, index, step, count):
-    return index ^ step if XOR[name] else lax.rem(index + count - step, count)
-
-
-def exchange(name, x, axes, step, count):
-    power = XOR[name]
-    pairs = [(i, i ^ step if power else (i + step) % count) for i in range(count)]
+    return index ^ step if paired(name, count) else lax.rem(index + count - step, count)
+
+
+def exchange(name, x, axes, step, count, inner=1, turn=0):
+    pairs = []
+    for i in range(count):
+        to = i ^ step if paired(name, count) else (i + step) % count
+        pairs += [(i * inner + c, to * inner + (c + turn) % inner) for c in range(inner)]
     return lax.ppermute(x, axes, pairs)
 
 
@@ -162,19 +168,17 @@
                 outs[k][at : at + rows, :] = sums_ref[c, q, pl.ds(to, rows), :]
 
 
-def place_kernel(count, blks, subs, spans, own, label_ref, *refs):
+def place_kernel(count, blks, subs, spans, own, label_ref, other_ref, *refs):
     parts, outs, total_ref = refs[:count], refs[count:-1], refs[-1]
     me = lax.axis_index("det")
     blocks, lanes = total_ref.shape[1:]
-    here = lax.axis_index("blk") * subs + lax.axis_index("sub")
-    number = lax.broadcasted_iota(jnp.int32, (blocks, lanes), 0)
-    masks = [
-        [
-            number == label_ref[pl.ds(source("bins", me, k, count) * spans + c, blocks, stride=0), :]
-            for c in range(spans)
-        ]
-        for k in range(count)
-    ]
+    number = lax.broadcasted_iota(jnp.int32, (blocks, lanes), 0).astype(jnp.float32)
+    masks = []
+    for k in range(count):
+        labels, first = (other_ref if k else label_ref), source("bins", me, k, count) * spans
+        masks.append(
+            [number == labels[pl.ds(first + c, blocks, stride=0), :] for c in range(spans)]
+        )
     rows = 3 * subs * own
     for row in range(rows):
         terms = [
@@ -186,13 +190,14 @@
             terms = [sum(terms[i : i + 2]) for i in range(0, len(terms), 2)]
         total_ref[row] = terms[0]
     for step, out in enumerate(outs):
-        to = partner("maps", here, step, blks * subs)
-        first, sub = to // subs * BLK_OWN, lax.rem(to, subs)
-        for q in range(3):
-            for r in range(own):
-                at = (q * own + r) * BLK_OWN
-                row = (q * subs + sub) * own + r
-                out[at : at + BLK_OWN, :] = total_ref[row, pl.ds(first, BLK_OWN), :]
+        first = partner("maps", lax.axis_index("blk"), step, blks) * BLK_OWN
+        for h in range(subs):
+            sub = lax.rem(lax.axis_index("sub") + (1 if step else 0) + h, subs)
+            for q in range(3):
+                for r in range(own):
+                    at = ((h * 3 + q) * own + r) * BLK_OWN
+                    row = (q * subs + sub) * own + r
+                    out[at : at + BLK_OWN, :] = total_ref[row, pl.ds(first, BLK_OWN), :]
 
 
 def on_device(tod, pixels, span_block, weight_class, class_weight):
@@ -235,19 +240,27 @@
         [VMEM] * (4 + dets),
         [held_index, pltpu.VMEM((spans, upper, lanes), f32)],
     )(weight, sums, half, row, *parts)
-    chunks = [chunks[0]] + [exchange("bins", chunks[k], "det", k, dets) for k in range(1, dets)]
-
-    peers = blks * subs
-    shape = jax.ShapeDtypeStruct((3 * own * BLK_OWN, lanes), f32)
+    label = span_block.reshape(-1, 1).astype(f32)
+    label = jnp.broadcast_to(label, (span_block.size, lanes))
+    other = exchange("label", label, ("det", "sub"), 0, dets, subs, 1)
+    chunks = [chunks[0]] + [
+        exchange("bins", chunks[k], ("det", "sub"), k, dets, subs, -1) for k in range(1, dets)
+    ]
+
+    shape = jax.ShapeDtypeStruct((subs * 3 * own * BLK_OWN, lanes), f32)
     placed = call(
         functools.partial(place_kernel, dets, blks, subs, spans, own),
-        [shape] * peers,
-        [VMEM] * (1 + dets),
+        [shape] * blks,
+        [VMEM] * (2 + dets),
         [pltpu.VMEM((3 * rows, BLK_OWN * blks, lanes), f32)],
-    )(jnp.broadcast_to(span_block.reshape(-1, 1), (span_block.size, lanes)), *chunks)
+    )(label, other, *chunks)
     total = placed[0]
-    for k in range(1, peers):
-        total = total + exchange("maps", placed[k], ("blk", "sub"), k, peers)
+    for k in range(1, blks):
+        total = total + exchange("maps", placed[k], ("blk", "sub"), k, blks, subs, 1)
+    shares = jnp.split(total, subs)
+    total = shares[0]
+    for h in range(1, subs):
+        total = total + exchange(f"swap{h}", shares[h], ("blk", "sub"), 0, blks, subs, h)
     total = total.reshape(3, own, BLK_OWN, lanes).transpose(0, 2, 1, 3)
     total = total.reshape(3, BLK_OWN, width)
     return total[0], total[1], total[2]

time: 26.4 us -> 25.4 us (0.962)
  waiting for transfers between devices: 8.68 us -> 7.33 us
  starting transfers between devices: 11.4 us -> 11.8 us
    ppermute x9, waiting for transfers between devices: 8.68 us -> 7.33 us  [exchange(): return lax.ppermute(x, axes, pairs)]
    ppermute x9, starting transfers between devices: 11.4 us -> 11.8 us  [exchange(): return lax.ppermute(x, axes, pairs)]
    unnamed x12 -> x11, local copies, waits for them, and re-layouts: 1.02 us -> 0.92 us
  transfers between devices with their start and end apart: 9 -> 9, of which waited for: 6 -> 5; matrix products, arithmetic and copies ran while one was open for 1% -> 2% of each run, Pallas kernels for 7% -> 7%
where the time goes in v4:
time: 25.4 us; the launch traced here: 25.2 us
  starting transfers between devices  11.8 us (46%)
  waiting for transfers between devices  7.33 us (29%)
  Pallas kernels  3.43 us (14%)
  local copies, waits for them, and re-layouts  1.88 us (7%)
  between operations  0.7 us (3%)
    ppermute x9, starting transfers between devices, exchange(): return lax.ppermute(x, axes, pairs)  11.8 us
    ppermute x9, waiting for transfers between devices, exchange(): return lax.ppermute(x, axes, pairs)  7.33 us
    pallas_call x1, Pallas kernels, on_device(): call(functools.partial(ahead_kernel, lanes, upper, group), [jax.ShapeDtyp...  1.88 us
    pallas_call x1, Pallas kernels, on_device(): call(functools.partial(value_kernel, dets, lanes, upper, rows, group), [s...  1.41 us
    unnamed x11, local copies, waits for them, and re-layouts  0.92 us
    squeeze x1, local copies, waits for them, and re-layouts, on_device(): return (total[0], total[1], total[2])  0.6 us
  transfers between devices with their start and end apart: 9, of which 5 were waited for; matrix products, arithmetic and copies ran while one was open for 2% of the time, Pallas kernels for 7%

profile of v4, /device:TPU:0, one launch (start us, length us, event | category | flops | bytes accessed | tf_op | source)
XLA Modules:
  0.0 25.2 jit_solution(16548823747441250566)
XLA Ops:
  0.6 0.0 copy-start
  0.6 0.9 %copy-done = f32[32,4,256]{2,1,0:T(4,128)S(1)} copy-done((f32[32,4,256]{2,1,0:T(4,128)S(1)}, f32[32,4,256]{2,1,0:T(4,128)}, u32[]{:S(2)}) %copy-start) | copy-done | bytes 131096
  1.5 0.0 copy-start.1
  1.5 0.1 shard_map.77
  1.6 3.1 %collective-permute-start.1 = (f32[32,256]{1,0:T(8,128)S(1)}, f32[32,256]{1,0:T(8,128)S(1)}, u32[]{:S(2)}, u32[]{:S(2)}) collective-permute-start(f32[32,256]{1,0:T(8,128)S(1)} %get-tuple-element.20), channel_id=1, source_target_pairs={{0,4},{4,0},{8,12},{12,8},{1,5},{5,1},{9,13},{13,9},{2,6},{6,2},{1... | collective-permute-start | bytes 98312 | tf_op jit(solution)/shard_map/ppermute | solution.py:35
  4.7 0.0 copy-start.3
  4.7 0.0 copy-start.4
  4.7 2.6 %collective-permute-start.2 = (f32[32,256]{1,0:T(8,128)S(1)}, f32[32,256]{1,0:T(8,128)S(1)}, u32[]{:S(2)}, u32[]{:S(2)}) collective-permute-start(f32[32,256]{1,0:T(8,128)S(1)} %get-tuple-element.21), channel_id=1, source_target_pairs={{0,8},{4,12},{8,0},{12,4},{1,9},{5,13},{9,1},{13,5},{2,10},{6,14},... | collective-permute-start | bytes 98312 | tf_op jit(solution)/shard_map/ppermute | solution.py:35
  7.3 0.0 collective-permute-start.3
  7.3 0.0 copy-done.3
  7.3 0.0 copy-done.4
  7.3 0.1 select_reduce_fusion
  7.4 0.0 copy-done.1
  7.4 0.1 broadcast_in_dim.5.weight_ref
  7.5 1.9 %shard_map.76 = (f32[2,2,24,128]{3,2,1,0:T(8,128)S(1)}, f32[2,128,128]{2,1,0:T(8,128)S(1)}, f32[2,128,128]{2,1,0:T(8,128)S(1)}) custom-call(s32[128,256]{1,0:T(8,128)S(1)} %bitcast.10, f32[128,128]{1,0:T(8,128)S(1)} %broadcast_in_dim.5.weight_ref), custom_call_target="tpu_custom_call" | custom-call | flops 1048576 | bytes 1048576 | tf_op jit(solution)/shard_map/pallas_call | solution.py:230
  9.4 0.0 collective-permute-done.1.refs_1_
  9.4 0.7 %collective-permute-done.2.refs_2_ = f32[32,256]{1,0:T(8,128)S(1)} collective-permute-done((f32[32,256]{1,0:T(8,128)S(1)}, f32[32,256]{1,0:T(8,128)S(1)}, u32[]{:S(2)}, u32[]{:S(2)}) %collective-permute-start.2) | collective-permute-done | bytes 32800 | tf_op jit(solution)/shard_map/ppermute | solution.py:35
  10.1 2.9 %collective-permute-done.3.refs_3_ = f32[32,256]{1,0:T(8,128)S(1)} collective-permute-done((f32[32,256]{1,0:T(8,128)S(1)}, f32[32,256]{1,0:T(8,128)S(1)}, u32[]{:S(2)}, u32[]{:S(2)}) %collective-permute-start.3) | collective-permute-done | bytes 32800 | tf_op jit(solution)/shard_map/ppermute | solution.py:35
  13.0 1.4 %shard_map.78 = (f32[36,128]{1,0:T(8,128)S(1)}, f32[36,128]{1,0:T(8,128)S(1)}, f32[36,128]{1,0:T(8,128)S(1)}, f32[36,128]{1,0:T(8,128)S(1)}) custom-call(f32[128,128]{1,0:T(8,128)S(1)} %broadcast_in_dim.5.weight_ref, f32[2,2,24,128]{3,2,1,0:T(8,128)S(1)} %get-tuple-element.16.sums_ref, f32[2,128,128]{2,1,0:T(8,128)S(1)} %get-tuple-element.17.half_ref, ...), custom_call_target="tpu_custom_call" | custom-call | flops 1048576 | bytes 1048576 | tf_op jit(solution)/shard_map/pallas_call | solution.py:237
  14.4 0.0 collective-permute-start.4
  14.5 0.0 copy-start.2
  14.5 0.6 %collective-permute-start.5 = (f32[36,128]{1,0:T(8,128)S(1)}, f32[36,128]{1,0:T(8,128)S(1)}, u32[]{:S(2)}, u32[]{:S(2)}) collective-permute-start(f32[36,128]{1,0:T(8,128)S(1)} %get-tuple-element.25), channel_id=1, source_target_pairs={{0,9},{1,8},{4,13},{5,12},{8,1},{9,0},{12,5},{13,4},{2,11},{3,10},... | collective-permute-start | bytes 55304 | tf_op jit(solution)/shard_map/ppermute | solution.py:35
  15.1 2.9 %collective-permute-start.6 = (f32[36,128]{1,0:T(8,128)S(1)}, f32[36,128]{1,0:T(8,128)S(1)}, u32[]{:S(2)}, u32[]{:S(2)}) collective-permute-start(f32[36,128]{1,0:T(8,128)S(1)} %get-tuple-element.26), channel_id=1, source_target_pairs={{0,13},{1,12},{4,1},{5,0},{8,5},{9,4},{12,9},{13,8},{2,15},{3,14},... | collective-permute-start | bytes 55304 | tf_op jit(solution)/shard_map/ppermute | solution.py:35
  18.0 0.0 copy-done.2
  18.0 0.1 copy.13
  18.1 0.1 convert_element_type.13
  18.2 0.1 broadcast_in_dim.4.label_ref
  18.3 0.0 collective-permute-start
  18.3 1.2 %collective-permute-done.other_ref = f32[8,128]{1,0:T(8,128)S(1)} collective-permute-done((f32[8,128]{1,0:T(8,128)S(1)}, f32[8,128]{1,0:T(8,128)S(1)}, u32[]{:S(2)}, u32[]{:S(2)}) %collective-permute-start) | collective-permute-done | bytes 4128 | tf_op jit(solution)/shard_map/ppermute | solution.py:35
  19.4 0.0 collective-permute-done.4.refs_1_
  19.5 0.0 collective-permute-done.5.refs_2_
  19.5 0.0 collective-permute-done.6.refs_3_
  19.5 0.1 shard_map.79
  19.6 1.8 %collective-permute-start.7 = (f32[72,128]{1,0:T(8,128)S(1)}, f32[72,128]{1,0:T(8,128)S(1)}, u32[]{:S(2)}, u32[]{:S(2)}) collective-permute-start(f32[72,128]{1,0:T(8,128)S(1)} %get-tuple-element.28), channel_id=1, source_target_pairs={{0,3},{1,2},{2,1},{3,0},{4,7},{5,6},{6,5},{7,4},{8,11},{9,10},{10,... | collective-permute-start | bytes 110600 | tf_op jit(solution)/shard_map/ppermute | solution.py:35
  21.4 1.6 %collective-permute-done.7 = f32[72,128]{1,0:T(8,128)S(1)} collective-permute-done((f32[72,128]{1,0:T(8,128)S(1)}, f32[72,128]{1,0:T(8,128)S(1)}, u32[]{:S(2)}, u32[]{:S(2)}) %collective-permute-start.7) | collective-permute-done | bytes 36896 | tf_op jit(solution)/shard_map/ppermute | solution.py:35
  23.0 0.7 %collective-permute-start.8 = (f32[36,128]{1,0:T(8,128)S(1)}, f32[36,128]{1,0:T(8,128)S(1)}, u32[]{:S(2)}, u32[]{:S(2)}) collective-permute-start(f32[36,128]{1,0:T(8,128)S(1)} %split.9), channel_id=1, source_target_pairs={{0,1},{1,0},{2,3},{3,2},{4,5},{5,4},{6,7},{7,6},{8,9},{9,8},{10,11... | collective-permute-start | bytes 55304 | tf_op jit(solution)/shard_map/ppermute | solution.py:35
  23.8 0.8 %collective-permute-done.8 = f32[36,128]{1,0:T(8,128)S(1)} collective-permute-done((f32[36,128]{1,0:T(8,128)S(1)}, f32[36,128]{1,0:T(8,128)S(1)}, u32[]{:S(2)}, u32[]{:S(2)}) %collective-permute-start.8) | collective-permute-done | bytes 18464 | tf_op jit(solution)/shard_map/ppermute | solution.py:35
  24.6 0.6 %slice_bitcast_fusion = (f32[4,384]{1,0:T(4,128)}, f32[4,384]{1,0:T(4,128)}, f32[4,384]{1,0:T(4,128)}) fusion(f32[3,4,3,128]{3,1,2,0:T(4,128)S(1)} %bitcast.11), kind=kLoop, calls=%fused_computation.2 | loop fusion | bytes 36864 | tf_op jit(solution)/shard_map/squeeze | solution.py:266
  (6 shorter events, 0.0 us)
Async XLA Ops:
  0.6 0.9 %copy-start = (f32[32,4,256]{2,1,0:T(4,128)S(1)}, f32[32,4,256]{2,1,0:T(4,128)}, u32[]{:S(2)}) copy-start(f32[32,4,256]{2,1,0:T(4,128)} %tod_ref.1) | copy-start | bytes 393220
  1.5 5.9 %copy-start.1 = (s32[128,1,256]{2,1,0:T(1,128)S(1)}, s32[128,1,256]{2,1,0:T(1,128)}, u32[]{:S(2)}) copy-start(s32[128,1,256]{2,1,0:T(1,128)} %param.6) | copy-start | bytes 393220
  1.6 7.8 %collective-permute-start.1 = (f32[32,256]{1,0:T(8,128)S(1)}, f32[32,256]{1,0:T(8,128)S(1)}, u32[]{:S(2)}, u32[]{:S(2)}) collective-permute-start(f32[32,256]{1,0:T(8,128)S(1)} %get-tuple-element.20), channel_id=1, source_target_pairs={{0,4},{4,0},{8,12},{12,8},{1,5},{5,1},{9,13},{13,9},{2,6},{6,2},{1... | collective-permute-start | bytes 98312 | tf_op jit(solution)/shard_map/ppermute | solution.py:35
  4.7 2.6 %copy-start.3 = (f32[8]{0:T(128)S(1)}, f32[8]{0:T(128)}, u32[]{:S(2)}) copy-start(f32[8]{0:T(128)} %param.9) | copy-start | bytes 100
  4.7 2.6 %copy-start.4 = (s32[128]{0:T(128)S(1)}, s32[128]{0:T(128)}, u32[]{:S(2)}) copy-start(s32[128]{0:T(128)} %param.8) | copy-start | bytes 1540
  4.7 5.4 %collective-permute-start.2 = (f32[32,256]{1,0:T(8,128)S(1)}, f32[32,256]{1,0:T(8,128)S(1)}, u32[]{:S(2)}, u32[]{:S(2)}) collective-permute-start(f32[32,256]{1,0:T(8,128)S(1)} %get-tuple-element.21), channel_id=1, source_target_pairs={{0,8},{4,12},{8,0},{12,4},{1,9},{5,13},{9,1},{13,5},{2,10},{6,14},... | collective-permute-start | bytes 98312 | tf_op jit(solution)/shard_map/ppermute | solution.py:35
  7.3 5.7 %collective-permute-start.3 = (f32[32,256]{1,0:T(8,128)S(1)}, f32[32,256]{1,0:T(8,128)S(1)}, u32[]{:S(2)}, u32[]{:S(2)}) collective-permute-start(f32[32,256]{1,0:T(8,128)S(1)} %get-tuple-element.22), channel_id=1, source_target_pairs={{0,12},{4,8},{8,4},{12,0},{1,13},{5,9},{9,5},{13,1},{2,14},{6,10},... | collective-permute-start | bytes 98312 | tf_op jit(solution)/shard_map/ppermute | solution.py:35
  14.4 5.0 %collective-permute-start.4 = (f32[36,128]{1,0:T(8,128)S(1)}, f32[36,128]{1,0:T(8,128)S(1)}, u32[]{:S(2)}, u32[]{:S(2)}) collective-permute-start(f32[36,128]{1,0:T(8,128)S(1)} %get-tuple-element.24), channel_id=1, source_target_pairs={{0,5},{1,4},{4,9},{5,8},{8,13},{9,12},{12,1},{13,0},{2,7},{3,6},{6... | collective-permute-start | bytes 55304 | tf_op jit(solution)/shard_map/ppermute | solution.py:35
  14.5 3.5 %copy-start.2 = (s32[4,2]{0,1:T(2,128)S(1)}, s32[4,2]{0,1:T(2,128)}, u32[]{:S(2)}) copy-start(s32[4,2]{0,1:T(2,128)} %param.7) | copy-start | bytes 100
  14.5 5.0 %collective-permute-start.5 = (f32[36,128]{1,0:T(8,128)S(1)}, f32[36,128]{1,0:T(8,128)S(1)}, u32[]{:S(2)}, u32[]{:S(2)}) collective-permute-start(f32[36,128]{1,0:T(8,128)S(1)} %get-tuple-element.25), channel_id=1, source_target_pairs={{0,9},{1,8},{4,13},{5,12},{8,1},{9,0},{12,5},{13,4},{2,11},{3,10},... | collective-permute-start | bytes 55304 | tf_op jit(solution)/shard_map/ppermute | solution.py:35
  15.1 4.4 %collective-permute-start.6 = (f32[36,128]{1,0:T(8,128)S(1)}, f32[36,128]{1,0:T(8,128)S(1)}, u32[]{:S(2)}, u32[]{:S(2)}) collective-permute-start(f32[36,128]{1,0:T(8,128)S(1)} %get-tuple-element.26), channel_id=1, source_target_pairs={{0,13},{1,12},{4,1},{5,0},{8,5},{9,4},{12,9},{13,8},{2,15},{3,14},... | collective-permute-start | bytes 55304 | tf_op jit(solution)/shard_map/ppermute | solution.py:35
  18.3 1.2 %collective-permute-start = (f32[8,128]{1,0:T(8,128)S(1)}, f32[8,128]{1,0:T(8,128)S(1)}, u32[]{:S(2)}, u32[]{:S(2)}) collective-permute-start(f32[8,128]{1,0:T(8,128)S(1)} %broadcast_in_dim.4.label_ref), channel_id=1, source_target_pairs={{0,1},{1,0},{4,5},{5,4},{8,9},{9,8},{12,13},{13,12},{2,3},{3,2},{6... | collective-permute-start | bytes 12296 | tf_op jit(solution)/shard_map/ppermute | solution.py:35
  19.6 3.5 %collective-permute-start.7 = (f32[72,128]{1,0:T(8,128)S(1)}, f32[72,128]{1,0:T(8,128)S(1)}, u32[]{:S(2)}, u32[]{:S(2)}) collective-permute-start(f32[72,128]{1,0:T(8,128)S(1)} %get-tuple-element.28), channel_id=1, source_target_pairs={{0,3},{1,2},{2,1},{3,0},{4,7},{5,6},{6,5},{7,4},{8,11},{9,10},{10,... | collective-permute-start | bytes 110600 | tf_op jit(solution)/shard_map/ppermute | solution.py:35
  23.0 1.6 %collective-permute-start.8 = (f32[36,128]{1,0:T(8,128)S(1)}, f32[36,128]{1,0:T(8,128)S(1)}, u32[]{:S(2)}, u32[]{:S(2)}) collective-permute-start(f32[36,128]{1,0:T(8,128)S(1)} %split.9), channel_id=1, source_target_pairs={{0,1},{1,0},{2,3},{3,2},{4,5},{5,4},{6,7},{7,6},{8,9},{9,8},{10,11... | collective-permute-start | bytes 55304 | tf_op jit(solution)/shard_map/ppermute | solution.py:35

commit v5 on v3

--- a/solution.py
+++ b/solution.py
@@ -190,9 +190,8 @@
         first, sub = to // subs * BLK_OWN, lax.rem(to, subs)
         for q in range(3):
             for r in range(own):
-                at = (q * own + r) * BLK_OWN
                 row = (q * subs + sub) * own + r
-                out[at : at + BLK_OWN, :] = total_ref[row, pl.ds(first, BLK_OWN), :]
+                out[q * own + r] = total_ref[row, pl.ds(first, BLK_OWN), :]
 
 
 def on_device(tod, pixels, span_block, weight_class, class_weight):
@@ -238,7 +237,7 @@
     chunks = [chunks[0]] + [exchange("bins", chunks[k], "det", k, dets) for k in range(1, dets)]
 
     peers = blks * subs
-    shape = jax.ShapeDtypeStruct((3 * own * BLK_OWN, lanes), f32)
+    shape = jax.ShapeDtypeStruct((3 * own, BLK_OWN, lanes), f32)
     placed = call(
         functools.partial(place_kernel, dets, blks, subs, spans, own),
         [shape] * peers,

time: 26.4 us -> 26.3 us (level)
  no operation moved by 1% of the time
where the time goes in v5:
time: 26.3 us; the launch traced here: 26.2 us
  starting transfers between devices  11.4 us (43%)
  waiting for transfers between devices  8.66 us (33%)
  Pallas kernels  3.43 us (13%)
  local copies, waits for them, and re-layouts  1.85 us (7%)
  between operations  0.71 us (3%)
    ppermute x9, starting transfers between devices, exchange(): return lax.ppermute(x, axes, pairs)  11.4 us
    ppermute x9, waiting for transfers between devices, exchange(): return lax.ppermute(x, axes, pairs)  8.66 us
    pallas_call x1, Pallas kernels, on_device(): call(functools.partial(ahead_kernel, lanes, upper, group), [jax.ShapeDtyp...  1.88 us
    pallas_call x1, Pallas kernels, on_device(): call(functools.partial(value_kernel, dets, lanes, upper, rows, group), [s...  1.41 us
    unnamed x12, local copies, waits for them, and re-layouts  1.02 us
    squeeze x1, local copies, waits for them, and re-layouts, on_device(): return (total[0], total[1], total[2])  0.6 us
  transfers between devices with their start and end apart: 9, of which 6 were waited for; matrix products, arithmetic and copies ran while one was open for 1% of the time, Pallas kernels for 7%

profile of v5, /device:TPU:0, one launch (start us, length us, event | category | flops | bytes accessed | tf_op | source)
XLA Modules:
  0.0 26.2 jit_solution(2196103913340694308)
XLA Ops:
  0.6 0.0 copy-start
  0.6 0.9 %copy-done = f32[32,4,256]{2,1,0:T(4,128)S(1)} copy-done((f32[32,4,256]{2,1,0:T(4,128)S(1)}, f32[32,4,256]{2,1,0:T(4,128)}, u32[]{:S(2)}) %copy-start) | copy-done | bytes 131096
  1.5 0.0 copy-start.1
  1.5 0.1 shard_map.77
  1.6 3.1 %collective-permute-start = (f32[32,256]{1,0:T(8,128)S(1)}, f32[32,256]{1,0:T(8,128)S(1)}, u32[]{:S(2)}, u32[]{:S(2)}) collective-permute-start(f32[32,256]{1,0:T(8,128)S(1)} %get-tuple-element.22), channel_id=1, source_target_pairs={{0,4},{4,0},{8,12},{12,8},{1,5},{5,1},{9,13},{13,9},{2,6},{6,2},{1... | collective-permute-start | bytes 98312 | tf_op jit(solution)/shard_map/ppermute | solution.py:29
  4.7 0.0 copy-start.3
  4.7 0.0 copy-start.4
  4.7 2.6 %collective-permute-start.1 = (f32[32,256]{1,0:T(8,128)S(1)}, f32[32,256]{1,0:T(8,128)S(1)}, u32[]{:S(2)}, u32[]{:S(2)}) collective-permute-start(f32[32,256]{1,0:T(8,128)S(1)} %get-tuple-element.23), channel_id=1, source_target_pairs={{0,8},{4,12},{8,0},{12,4},{1,9},{5,13},{9,1},{13,5},{2,10},{6,14},... | collective-permute-start | bytes 98312 | tf_op jit(solution)/shard_map/ppermute | solution.py:29
  7.3 0.0 collective-permute-start.2
  7.3 0.0 copy-done.3
  7.3 0.0 copy-done.4
  7.3 0.1 select_reduce_fusion
  7.4 0.0 copy-done.1
  7.4 0.1 broadcast_in_dim.8.weight_ref
  7.5 1.9 %shard_map.76 = (f32[2,2,24,128]{3,2,1,0:T(8,128)S(1)}, f32[2,128,128]{2,1,0:T(8,128)S(1)}, f32[2,128,128]{2,1,0:T(8,128)S(1)}) custom-call(s32[128,256]{1,0:T(8,128)S(1)} %bitcast.12, f32[128,128]{1,0:T(8,128)S(1)} %broadcast_in_dim.8.weight_ref), custom_call_target="tpu_custom_call" | custom-call | flops 1048576 | bytes 1048576 | tf_op jit(solution)/shard_map/pallas_call | solution.py:224
  9.4 0.0 collective-permute-done.refs_1_
  9.4 0.7 %collective-permute-done.1.refs_2_ = f32[32,256]{1,0:T(8,128)S(1)} collective-permute-done((f32[32,256]{1,0:T(8,128)S(1)}, f32[32,256]{1,0:T(8,128)S(1)}, u32[]{:S(2)}, u32[]{:S(2)}) %collective-permute-start.1) | collective-permute-done | bytes 32800 | tf_op jit(solution)/shard_map/ppermute | solution.py:29
  10.1 2.9 %collective-permute-done.2.refs_3_ = f32[32,256]{1,0:T(8,128)S(1)} collective-permute-done((f32[32,256]{1,0:T(8,128)S(1)}, f32[32,256]{1,0:T(8,128)S(1)}, u32[]{:S(2)}, u32[]{:S(2)}) %collective-permute-start.2) | collective-permute-done | bytes 32800 | tf_op jit(solution)/shard_map/ppermute | solution.py:29
  13.0 1.4 %shard_map.78 = (f32[36,128]{1,0:T(8,128)S(1)}, f32[36,128]{1,0:T(8,128)S(1)}, f32[36,128]{1,0:T(8,128)S(1)}, f32[36,128]{1,0:T(8,128)S(1)}) custom-call(f32[128,128]{1,0:T(8,128)S(1)} %broadcast_in_dim.8.weight_ref, f32[2,2,24,128]{3,2,1,0:T(8,128)S(1)} %get-tuple-element.18.sums_ref, f32[2,128,128]{2,1,0:T(8,128)S(1)} %get-tuple-element.19.half_ref, ...), custom_call_target="tpu_custom_call" | custom-call | flops 1048576 | bytes 1048576 | tf_op jit(solution)/shard_map/pallas_call | solution.py:231
  14.4 0.0 collective-permute-start.3
  14.5 0.0 copy-start.2
  14.5 0.9 %collective-permute-start.4 = (f32[36,128]{1,0:T(8,128)S(1)}, f32[36,128]{1,0:T(8,128)S(1)}, u32[]{:S(2)}, u32[]{:S(2)}) collective-permute-start(f32[36,128]{1,0:T(8,128)S(1)} %get-tuple-element.27), channel_id=1, source_target_pairs={{0,8},{4,12},{8,0},{12,4},{1,9},{5,13},{9,1},{13,5},{2,10},{6,14},... | collective-permute-start | bytes 55304 | tf_op jit(solution)/shard_map/ppermute | solution.py:29
  15.4 2.9 %collective-permute-start.5 = (f32[36,128]{1,0:T(8,128)S(1)}, f32[36,128]{1,0:T(8,128)S(1)}, u32[]{:S(2)}, u32[]{:S(2)}) collective-permute-start(f32[36,128]{1,0:T(8,128)S(1)} %get-tuple-element.28), channel_id=1, source_target_pairs={{0,12},{4,0},{8,4},{12,8},{1,13},{5,1},{9,5},{13,9},{2,14},{6,2},{... | collective-permute-start | bytes 55304 | tf_op jit(solution)/shard_map/ppermute | solution.py:29
  18.3 0.0 copy-done.2
  18.3 0.1 copy.13
  18.4 0.1 broadcast_in_dim.6
  18.5 1.6 %collective-permute-done.3.refs_1_ = f32[36,128]{1,0:T(8,128)S(1)} collective-permute-done((f32[36,128]{1,0:T(8,128)S(1)}, f32[36,128]{1,0:T(8,128)S(1)}, u32[]{:S(2)}, u32[]{:S(2)}) %collective-permute-start.3) | collective-permute-done | bytes 18464 | tf_op jit(solution)/shard_map/ppermute | solution.py:29
  20.0 0.0 collective-permute-done.4.refs_2_
  20.0 0.6 %collective-permute-done.5.refs_3_ = f32[36,128]{1,0:T(8,128)S(1)} collective-permute-done((f32[36,128]{1,0:T(8,128)S(1)}, f32[36,128]{1,0:T(8,128)S(1)}, u32[]{:S(2)}, u32[]{:S(2)}) %collective-permute-start.5) | collective-permute-done | bytes 18464 | tf_op jit(solution)/shard_map/ppermute | solution.py:29
  20.6 0.1 broadcast_in_dim.7.label_ref
  20.7 0.1 shard_map.79
  20.8 0.1 collective-permute-start.6
  20.8 1.6 %collective-permute-start.7 = (f32[9,4,128]{2,1,0:T(4,128)S(1)}, f32[9,4,128]{2,1,0:T(4,128)S(1)}, u32[]{:S(2)}, u32[]{:S(2)}) collective-permute-start(f32[9,4,128]{2,1,0:T(4,128)S(1)} %get-tuple-element.31), channel_id=1, source_target_pairs={{0,2},{1,3},{2,0},{3,1},{4,6},{5,7},{6,4},{7,5},{8,10},{9,11},{10,... | collective-permute-start | bytes 55304 | tf_op jit(solution)/shard_map/ppermute | solution.py:29
  22.4 0.3 %collective-permute-start.8 = (f32[9,4,128]{2,1,0:T(4,128)S(1)}, f32[9,4,128]{2,1,0:T(4,128)S(1)}, u32[]{:S(2)}, u32[]{:S(2)}) collective-permute-start(f32[9,4,128]{2,1,0:T(4,128)S(1)} %get-tuple-element.32), channel_id=1, source_target_pairs={{0,3},{1,2},{2,1},{3,0},{4,7},{5,6},{6,5},{7,4},{8,11},{9,10},{10,... | collective-permute-start | bytes 55304 | tf_op jit(solution)/shard_map/ppermute | solution.py:29
  22.7 0.0 collective-permute-done.6
  22.7 2.0 %collective-permute-done.7 = f32[9,4,128]{2,1,0:T(4,128)S(1)} collective-permute-done((f32[9,4,128]{2,1,0:T(4,128)S(1)}, f32[9,4,128]{2,1,0:T(4,128)S(1)}, u32[]{:S(2)}, u32[]{:S(2)}) %collective-permute-start.7) | collective-permute-done | bytes 18464 | tf_op jit(solution)/shard_map/ppermute | solution.py:29
  24.7 0.9 %collective-permute-done.8 = f32[9,4,128]{2,1,0:T(4,128)S(1)} collective-permute-done((f32[9,4,128]{2,1,0:T(4,128)S(1)}, f32[9,4,128]{2,1,0:T(4,128)S(1)}, u32[]{:S(2)}, u32[]{:S(2)}) %collective-permute-start.8) | collective-permute-done | bytes 18464 | tf_op jit(solution)/shard_map/ppermute | solution.py:29
  25.6 0.6 %slice_bitcast_fusion = (f32[4,384]{1,0:T(4,128)}, f32[4,384]{1,0:T(4,128)}, f32[4,384]{1,0:T(4,128)}) fusion(f32[3,4,3,128]{3,1,2,0:T(4,128)S(1)} %bitcast.13), kind=kLoop, calls=%fused_computation.2 | loop fusion | bytes 36864 | tf_op jit(solution)/shard_map/squeeze | solution.py:252
  (2 shorter events, 0.0 us)
Async XLA Ops:
  0.6 0.9 %copy-start = (f32[32,4,256]{2,1,0:T(4,128)S(1)}, f32[32,4,256]{2,1,0:T(4,128)}, u32[]{:S(2)}) copy-start(f32[32,4,256]{2,1,0:T(4,128)} %tod_ref.1) | copy-start | bytes 393220
  1.5 5.9 %copy-start.1 = (s32[128,1,256]{2,1,0:T(1,128)S(1)}, s32[128,1,256]{2,1,0:T(1,128)}, u32[]{:S(2)}) copy-start(s32[128,1,256]{2,1,0:T(1,128)} %param.6) | copy-start | bytes 393220
  1.6 7.8 %collective-permute-start = (f32[32,256]{1,0:T(8,128)S(1)}, f32[32,256]{1,0:T(8,128)S(1)}, u32[]{:S(2)}, u32[]{:S(2)}) collective-permute-start(f32[32,256]{1,0:T(8,128)S(1)} %get-tuple-element.22), channel_id=1, source_target_pairs={{0,4},{4,0},{8,12},{12,8},{1,5},{5,1},{9,13},{13,9},{2,6},{6,2},{1... | collective-permute-start | bytes 98312 | tf_op jit(solution)/shard_map/ppermute | solution.py:29
  4.7 2.6 %copy-start.3 = (f32[8]{0:T(128)S(1)}, f32[8]{0:T(128)}, u32[]{:S(2)}) copy-start(f32[8]{0:T(128)} %param.9) | copy-start | bytes 100
  4.7 2.6 %copy-start.4 = (s32[128]{0:T(128)S(1)}, s32[128]{0:T(128)}, u32[]{:S(2)}) copy-start(s32[128]{0:T(128)} %param.8) | copy-start | bytes 1540
  4.7 5.4 %collective-permute-start.1 = (f32[32,256]{1,0:T(8,128)S(1)}, f32[32,256]{1,0:T(8,128)S(1)}, u32[]{:S(2)}, u32[]{:S(2)}) collective-permute-start(f32[32,256]{1,0:T(8,128)S(1)} %get-tuple-element.23), channel_id=1, source_target_pairs={{0,8},{4,12},{8,0},{12,4},{1,9},{5,13},{9,1},{13,5},{2,10},{6,14},... | collective-permute-start | bytes 98312 | tf_op jit(solution)/shard_map/ppermute | solution.py:29
  7.3 5.7 %collective-permute-start.2 = (f32[32,256]{1,0:T(8,128)S(1)}, f32[32,256]{1,0:T(8,128)S(1)}, u32[]{:S(2)}, u32[]{:S(2)}) collective-permute-start(f32[32,256]{1,0:T(8,128)S(1)} %get-tuple-element.24), channel_id=1, source_target_pairs={{0,12},{4,8},{8,4},{12,0},{1,13},{5,9},{9,5},{13,1},{2,14},{6,10},... | collective-permute-start | bytes 98312 | tf_op jit(solution)/shard_map/ppermute | solution.py:29
  14.4 5.6 %collective-permute-start.3 = (f32[36,128]{1,0:T(8,128)S(1)}, f32[36,128]{1,0:T(8,128)S(1)}, u32[]{:S(2)}, u32[]{:S(2)}) collective-permute-start(f32[36,128]{1,0:T(8,128)S(1)} %get-tuple-element.26), channel_id=1, source_target_pairs={{0,4},{4,8},{8,12},{12,0},{1,5},{5,9},{9,13},{13,1},{2,6},{6,10},{... | collective-permute-start | bytes 55304 | tf_op jit(solution)/shard_map/ppermute | solution.py:29
  14.5 3.8 %copy-start.2 = (s32[4,2]{0,1:T(2,128)S(1)}, s32[4,2]{0,1:T(2,128)}, u32[]{:S(2)}) copy-start(s32[4,2]{0,1:T(2,128)} %param.7) | copy-start | bytes 100
  14.5 5.6 %collective-permute-start.4 = (f32[36,128]{1,0:T(8,128)S(1)}, f32[36,128]{1,0:T(8,128)S(1)}, u32[]{:S(2)}, u32[]{:S(2)}) collective-permute-start(f32[36,128]{1,0:T(8,128)S(1)} %get-tuple-element.27), channel_id=1, source_target_pairs={{0,8},{4,12},{8,0},{12,4},{1,9},{5,13},{9,1},{13,5},{2,10},{6,14},... | collective-permute-start | bytes 55304 | tf_op jit(solution)/shard_map/ppermute | solution.py:29
  15.4 5.2 %collective-permute-start.5 = (f32[36,128]{1,0:T(8,128)S(1)}, f32[36,128]{1,0:T(8,128)S(1)}, u32[]{:S(2)}, u32[]{:S(2)}) collective-permute-start(f32[36,128]{1,0:T(8,128)S(1)} %get-tuple-element.28), channel_id=1, source_target_pairs={{0,12},{4,0},{8,4},{12,8},{1,13},{5,1},{9,5},{13,9},{2,14},{6,2},{... | collective-permute-start | bytes 55304 | tf_op jit(solution)/shard_map/ppermute | solution.py:29
  20.8 1.9 %collective-permute-start.6 = (f32[9,4,128]{2,1,0:T(4,128)S(1)}, f32[9,4,128]{2,1,0:T(4,128)S(1)}, u32[]{:S(2)}, u32[]{:S(2)}) collective-permute-start(f32[9,4,128]{2,1,0:T(4,128)S(1)} %get-tuple-element.30), channel_id=1, source_target_pairs={{0,1},{1,0},{2,3},{3,2},{4,5},{5,4},{6,7},{7,6},{8,9},{9,8},{10,11... | collective-permute-start | bytes 55304 | tf_op jit(solution)/shard_map/ppermute | solution.py:29
  20.8 3.8 %collective-permute-start.7 = (f32[9,4,128]{2,1,0:T(4,128)S(1)}, f32[9,4,128]{2,1,0:T(4,128)S(1)}, u32[]{:S(2)}, u32[]{:S(2)}) collective-permute-start(f32[9,4,128]{2,1,0:T(4,128)S(1)} %get-tuple-element.31), channel_id=1, source_target_pairs={{0,2},{1,3},{2,0},{3,1},{4,6},{5,7},{6,4},{7,5},{8,10},{9,11},{10,... | collective-permute-start | bytes 55304 | tf_op jit(solution)/shard_map/ppermute | solution.py:29
  22.4 3.2 %collective-permute-start.8 = (f32[9,4,128]{2,1,0:T(4,128)S(1)}, f32[9,4,128]{2,1,0:T(4,128)S(1)}, u32[]{:S(2)}, u32[]{:S(2)}) collective-permute-start(f32[9,4,128]{2,1,0:T(4,128)S(1)} %get-tuple-element.32), channel_id=1, source_target_pairs={{0,3},{1,2},{2,1},{3,0},{4,7},{5,6},{6,5},{7,4},{8,11},{9,10},{10,... | collective-permute-start | bytes 55304 | tf_op jit(solution)/shard_map/ppermute | solution.py:29
